TPU v7x, 256 devices: a whole 4x4x8 slice. The times are simulated.
256 devices in a mesh: gx: 8 (over y, core), gy: 32 (over z, x).
Axes of the slice: x: 4, y: 4, z: 8, core: 2. Of those that a mesh axis runs over, the one named last changes fastest.
Arguments:
- reference_image: bfloat16 [64, 128, 4096], P(None, 'gx', 'gy'), may hold values from -8 to 8
- deformed_image: bfloat16 [64, 128, 4096], P(None, 'gx', 'gy'), may hold values from -8 to 8
- route: int32 [8, 32, 32, 1], P('gx', 'gy'), may hold values from 0 to 4; in each aligned block of 32 rows (0 to 31, 32 to 63, ..., all dimensions but the last counted through in order) at most 8 rows name the same one
- within: int32 [8, 32, 32], P('gx', 'gy'), may hold values from 0 to 7
- xshift: int32 [8, 32, 32], P('gx', 'gy'), may hold values from 0 to 2
- fractions: int32 [8, 32, 32, 3], P('gx', 'gy'), may hold values from 0 to 15
Outputs:
- increment: float32 [3, 5, 8, 256], P(None, None, 'gx', 'gy')
- mismatch: float32 [64, 128, 4096], P(None, 'gx', 'gy')
Inputs may be any that keep to these rules, and one draw needn't show every extreme that they name: `route`: among the 32 rows of one device (aligned blocks of rows along the first three dimensions taken together) no value occurs more than 8 times, and some value occurs exactly 8 times.
All inputs are finite; a program needn't handle non-finite values.
Results may differ from a plain program's by a relative error of at most 0.0006.
Values may be sent and summed in bfloat16 or wider, within the bound.
A program may use at most 64 MiB of HBM per device.

v0:
```python
import jax
import jax.numpy as jnp
from jax import lax
from jax.sharding import PartitionSpec as P

EDGE = 16
EZ = 4
EXD = 1
EYD = 8
SPAN = 2
ITERS = 3
NEL = 32
VOL = 4096


LAMBDA = 0.05


def from_behind(array, axis, by):
    size = lax.axis_size(axis)
    pairs = [(i, i + by) for i in range(size) if 0 <= i + by < size]
    return lax.ppermute(array, axis, pairs)


def padded_2(block, sides, width):
    for axis, dim in sides:
        count = lax.axis_size(axis)
        forward = [(i, i + 1) for i in range(count - 1)]
        backward = [(target, source) for source, target in forward]
        low = lax.ppermute(
            lax.slice_in_dim(block, block.shape[dim] - width, None, axis=dim), axis, forward
        )
        high = lax.ppermute(lax.slice_in_dim(block, 0, width, axis=dim), axis, backward)
        block = jnp.concatenate([low, block, high], axis=dim)
    return block


def passed_along(block, axis, distance):
    devices = range(lax.axis_size(axis))
    route = [((i - distance) % len(devices), i) for i in devices]
    return lax.ppermute(block, axis, route)


def hat_positions(brick_edge, trailing):
    positions = (jnp.arange(brick_edge, dtype=jnp.float32) + 0.5) / brick_edge
    return positions.reshape((brick_edge,) + (1,) * trailing)


def spread_along(node_values, which_axis, brick_edge):
    node_count = node_values.shape[which_axis] - 1
    positions = hat_positions(brick_edge, node_values.ndim - which_axis - 1)
    lower_part = jnp.expand_dims(
        lax.slice_in_dim(node_values, 0, node_count, axis=which_axis), which_axis + 1
    )
    upper_part = jnp.expand_dims(
        lax.slice_in_dim(node_values, 1, node_count + 1, axis=which_axis), which_axis + 1
    )
    blended = lower_part * (1.0 - positions) + upper_part * positions
    new_shape = (
        node_values.shape[:which_axis]
        + (node_count * brick_edge,)
        + node_values.shape[which_axis + 1 :]
    )
    return blended.reshape(new_shape)


def collect_along(voxel_values, which_axis, brick_edge):
    node_count = voxel_values.shape[which_axis] // brick_edge
    positions = hat_positions(brick_edge, voxel_values.ndim - which_axis - 1)
    blocks = voxel_values.reshape(
        voxel_values.shape[:which_axis]
        + (node_count, brick_edge)
        + voxel_values.shape[which_axis + 1 :]
    )
    lower_part = jnp.sum(blocks * (1.0 - positions), axis=which_axis + 1)
    upper_part = jnp.sum(blocks * positions, axis=which_axis + 1)
    zero_cap = jnp.zeros_like(lax.slice_in_dim(lower_part, 0, 1, axis=which_axis))
    return jnp.concatenate([lower_part, zero_cap], which_axis) + jnp.concatenate(
        [zero_cap, upper_part], which_axis
    )


def clamp_shift(bricks, stride):
    advanced = jnp.concatenate([bricks[:, stride:], bricks[:, -stride:]], axis=1)
    places = jnp.arange(bricks.shape[1], dtype=jnp.int32)
    at_rim = places // stride % EDGE == EDGE - 1
    return jnp.where(at_rim[None, :], bricks, advanced)


def warp_bricks(bricks, fractions):
    weights = fractions.astype(jnp.float32) / EDGE
    blended = bricks
    for column, stride in ((2, 1), (1, EDGE), (0, EDGE * EDGE)):
        portion = weights[:, column : column + 1]
        blended = (1.0 - portion) * blended + portion * clamp_shift(blended, stride)
    return blended


def local_bricks(image, depth_count, width_count, height_count):
    shaped = image.reshape(depth_count, EDGE, width_count, EDGE, height_count, EDGE)
    return shaped.transpose(0, 2, 4, 1, 3, 5).reshape(depth_count * width_count * height_count, VOL)


def settle_faces(partial_value):
    upper_rim = partial_value[:, :, -1, :]
    arrived = from_behind(upper_rim, "gx", 1)
    interior = partial_value[:, :, :-1, :].at[:, :, 0, :].add(arrived)
    side_rim = interior[:, :, :, -1]
    arrived_side = from_behind(side_rim, "gy", 1)
    return interior[:, :, :, :-1].at[:, :, :, 0].add(arrived_side)


def reach_faces(unknown):
    next_row = from_behind(unknown, "gx", -1)
    wider = jnp.concatenate([unknown, next_row], axis=2)
    next_column = from_behind(wider[:, :, :, :1], "gy", -1)
    return jnp.concatenate([wider, next_column], axis=3)


def restrict(voxel_terms):
    partial_value = collect_along(
        collect_along(collect_along(voxel_terms, 1, EDGE), 2, EDGE), 3, EDGE
    )
    return settle_faces(partial_value) / VOL


def squared(vector):
    return lax.psum(jnp.sum(vector * vector), ("gx", "gy"))


def body(reference_image, deformed_image, route, within, xshift, fractions):
    column_x = lax.axis_index("gx")
    width_devices = lax.axis_size("gx")
    offsets = route.reshape(NEL) - SPAN
    within_rows = within.reshape(NEL)
    shift_rows = xshift.reshape(NEL)
    weights_rows = fractions.reshape(NEL, 3)
    element = jnp.arange(NEL, dtype=jnp.int32)
    depth_rows = element // (EXD * EYD)
    across = element // EYD % EXD
    global_x = column_x * EXD + across
    source_x = jnp.clip(global_x + shift_rows - 1, 0, EXD * width_devices - 1)
    local_x = source_x - column_x * EXD + 1
    source_index = (depth_rows * (EXD + 2) + local_x) * EYD + within_rows
    extended = padded_2(deformed_image, (("gx", 1),), EDGE)
    wide_rows = local_bricks(extended, EZ, EXD + 2, EYD)
    fetched = jnp.take(wide_rows, source_index, axis=0)
    for distance in range(-SPAN, SPAN + 1):
        if distance != 0:
            window = passed_along(wide_rows, "gy", -distance)
            picked = jnp.take(window, source_index, axis=0)
            fetched = jnp.where((offsets == distance)[:, None], picked, fetched)
    warped = warp_bricks(fetched.astype(jnp.float32), weights_rows)
    reference_rows = local_bricks(reference_image, EZ, EXD, EYD)
    mismatch_rows = reference_rows.astype(jnp.float32) - warped
    mismatch = (
        mismatch_rows.reshape(EZ, EXD, EYD, EDGE, EDGE, EDGE)
        .transpose(0, 3, 1, 4, 2, 5)
        .reshape(reference_image.shape)
    )
    padded = padded_2(reference_image, (("gx", 1), ("gy", 2)), 1)
    padded = jnp.pad(padded, ((1, 1), (0, 0), (0, 0)))
    middle = padded[1:-1].astype(jnp.float32)
    along_z = (
        padded[2:, 1:-1, 1:-1].astype(jnp.float32) - padded[:-2, 1:-1, 1:-1].astype(jnp.float32)
    ) * 0.5
    along_x = (middle[:, 2:, 1:-1] - middle[:, :-2, 1:-1]) * 0.5
    along_y = (middle[:, 1:-1, 2:] - middle[:, 1:-1, :-2]) * 0.5
    gradient = jnp.stack([along_z, along_x, along_y]).astype(jnp.bfloat16)
    residual = restrict(gradient.astype(jnp.float32) * mismatch[None])
    increment = jnp.zeros_like(residual)
    direction = residual
    norm_now = squared(residual)
    for iteration in range(ITERS):
        node_values = reach_faces(direction)
        displaced = spread_along(spread_along(spread_along(node_values, 3, EDGE), 2, EDGE), 1, EDGE)
        normal_part = jnp.sum(gradient.astype(jnp.float32) * displaced, axis=0)
        curved = restrict(gradient.astype(jnp.float32) * normal_part[None]) + LAMBDA * direction
        step_size = norm_now / lax.psum(jnp.sum(direction * curved), ("gx", "gy"))
        increment = increment + step_size * direction
        if iteration + 1 < ITERS:
            residual = residual - step_size * curved
            norm_next = squared(residual)
            direction = residual + norm_next / norm_now * direction
            norm_now = norm_next
    return (increment, mismatch)


def solution(mesh):
    placed = (
        P(None, "gx", "gy"),
        P(None, "gx", "gy"),
        P("gx", "gy", None, None),
        P("gx", "gy", None),
        P("gx", "gy", None),
        P("gx", "gy", None, None),
    )
    return jax.shard_map(
        body,
        mesh=mesh,
        in_specs=placed,
        out_specs=(P(None, None, "gx", "gy"), P(None, "gx", "gy")),
        check_vma=False,
    )
```

profile of v0, /device:TPU:1, one launch (start us, length us, event | category | flops | bytes accessed | tf_op | source)
XLA Modules:
  0.0 638.3 jit_solution(7497479306553021862)
XLA Ops:
  0.6 4.6 collective-permute-start.4
  5.2 1.9 collective-permute-start.5
  8.2 3.6 collective-permute-start
  11.8 1.9 collective-permute-start.1
  16.3 1.2 compare_and_fusion
  20.4 5.7 reshape.640
  26.1 7.2 %copy.179 = bf16[4,16,3,16,8,16]{5,3,1,4,2,0:T(8,128)(2,1)} copy(bf16[4,16,3,16,8,16]{5,4,3,2,1,0:T(8,128)(2,1)} %reshape.640) | data formatting | bytes 1572864 | tf_op jit(solution)/shard_map/reshape | solution.py:100
  33.3 11.6 %reshape.641 = bf16[96,4096]{1,0:T(8,128)(2,1)S(1)} reshape(bf16[4,3,8,16,16,16]{5,4,3,2,1,0:T(8,128)(2,1)} %bitcast.139) | data formatting | bytes 1572864 | tf_op jit(solution)/shard_map/reshape | solution.py:101
  45.0 8.1 %collective-permute-start.6 = (bf16[96,4096]{1,0:T(8,128)(2,1)S(1)}, bf16[96,4096]{1,0:T(8,128)(2,1)}, u32[]{:S(2)}, u32[]{:S(2)}) collective-permute-start(bf16[96,4096]{1,0:T(8,128)(2,1)S(1)} %reshape.641), channel_id=1, source_target_pairs={{2,0},{3,1},{4,2},{5,3},{6,4},{7,5},{8,6},{9,7},{10,8},{11,9},{12,... | collective-permute-start | bytes 2359304 | tf_op jit(solution)/shard_map/ppermute | solution.py:41
  55.4 1.6 collective-permute-start.2
  57.6 49.3 %collective-permute-done.2 = bf16[64,18,1]{2,1,0:T(8,128)(2,1)S(1)} collective-permute-done((bf16[64,18,1]{2,1,0:T(8,128)(2,1)S(1)}, bf16[64,18,1]{2,1,0:T(8,128)(2,1)S(1)}, u32[]{:S(2)}, u32[]{:S(2)}) %collective-permute-start.2) | collective-permute-done | bytes 2336 | tf_op jit(solution)/shard_map/ppermute | solution.py:30
  106.9 1.5 collective-permute-start.3
  108.4 2.5 reshape.660
  110.9 4.9 copy.181
  115.8 5.4 reshape.657
  121.2 1.7 fusion.60
  124.4 2.9 gather_fusion
  127.3 2.9 gather_fusion.1
  130.2 1.4 gather_fusion.2
  134.8 2.8 reshape.643
  137.6 6.5 %copy.180 = f32[4,1,8,16,16,16]{5,2,4,3,0,1:T(8,128)} copy(f32[4,1,8,16,16,16]{5,4,3,2,0,1:T(8,128)} %reshape.643) | data formatting | bytes 1048576 | tf_op jit(solution)/shard_map/reshape | solution.py:157
  144.2 3.2 mul.741
  148.3 4.8 collective-permute-start.10
  154.2 14.0 %collective-permute-start.11 = (f32[3,5,1]{1,2,0:T(1,128)S(1)}, f32[3,5,1]{1,2,0:T(1,128)S(1)}, u32[]{:S(2)}, u32[]{:S(2)}) collective-permute-start(f32[3,5,1]{1,2,0:T(1,128)S(1)} %squeeze.25), channel_id=1, source_target_pairs={{0,1},{1,2},{2,3},{3,4},{4,5},{5,6},{6,7},{7,8},{8,9},{9,10},{10,1... | collective-permute-start | bytes 188 | tf_op jit(solution)/shard_map/ppermute | solution.py:22
  169.4 1.9 collective-permute-start.12
  171.4 4.4 collective-permute-done.12
  175.8 1.3 collective-permute-start.13
  177.2 5.9 collective-permute-done.13
  185.2 2.8 collective-permute-start.14
  189.1 4.1 collective-permute-start.15
  194.8 88.4 %all-reduce.25 = (f32[]{:T(128)}, f32[]{:T(128)}) all-reduce(f32[]{:T(128)} %get-tuple-element.130, f32[]{:T(128)} %get-tuple-element.129), channel_id=1, replica_groups=mesh['gx'=8,'gy'=32] {'gx','gy'}, use_global_device_ids=true, to_apply=%region_7.9 | all-reduce | flops 2 | bytes 16 | tf_op jit(solution)/shard_map/psum | solution.py:128
  285.2 74.0 %psum.44 = f32[]{:T(128)} all-reduce(f32[]{:T(128)} %get-tuple-element.135), channel_id=1, replica_groups=mesh['gx'=8,'gy'=32] {'gx','gy'}, use_global_device_ids=true, to_apply=%region_18.20 | all-reduce | flops 1 | bytes 8 | tf_op jit(solution)/shard_map/psum | solution.py:128
  360.6 2.6 collective-permute-start.16
  363.2 2.4 collective-permute-done.16
  365.6 1.3 collective-permute-start.17
  366.9 3.2 collective-permute-done.17
  372.1 3.2 collective-permute-start.18
  376.4 2.5 collective-permute-start.19
  380.5 78.3 %psum.45 = f32[]{:T(128)} all-reduce(f32[]{:T(128)} %multiply_reduce_fusion.18), channel_id=1, replica_groups=mesh['gx'=8,'gy'=32] {'gx','gy'}, use_global_device_ids=true, to_apply=%region_27.29 | all-reduce | flops 1 | bytes 8 | tf_op jit(solution)/shard_map/psum | solution.py:179
  460.7 74.2 %psum.46 = f32[]{:T(128)} all-reduce(f32[]{:T(128)} %get-tuple-element.133), channel_id=1, replica_groups=mesh['gx'=8,'gy'=32] {'gx','gy'}, use_global_device_ids=true, to_apply=%region_29.31 | all-reduce | flops 1 | bytes 8 | tf_op jit(solution)/shard_map/psum | solution.py:128
  536.3 2.6 collective-permute-start.20
  538.9 2.4 collective-permute-done.20
  541.3 1.3 collective-permute-start.21
  542.6 3.2 collective-permute-done.21
  547.8 3.2 collective-permute-start.22
  552.1 2.3 collective-permute-start.23
  554.5 3.9 reshape.656
  559.3 77.0 %psum.47 = f32[]{:T(128)} all-reduce(f32[]{:T(128)} %multiply_reduce_fusion.16), channel_id=1, replica_groups=mesh['gx'=8,'gy'=32] {'gx','gy'}, use_global_device_ids=true, to_apply=%region_38.40 | all-reduce | flops 1 | bytes 8 | tf_op jit(solution)/shard_map/psum | solution.py:179
  (212 shorter events, 31.9 us)
Async XLA Ops:
  0.6 18.7 %collective-permute-start.4 = (bf16[64,16,128]{2,1,0:T(8,128)(2,1)}, bf16[64,16,128]{2,1,0:T(8,128)(2,1)S(1)}, u32[]{:S(2)}, u32[]{:S(2)}) collective-permute-start(bf16[64,16,128]{2,1,0:T(8,128)(2,1)} %param.25), channel_id=1, source_target_pairs={{0,32},{32,64},{64,96},{96,128},{128,160},{160,192},{192,224},{1,3... | collective-permute-start | bytes 786440 | tf_op jit(solution)/shard_map/ppermute | solution.py:30
  5.2 14.1 %collective-permute-start.5 = (bf16[64,16,128]{2,1,0:T(8,128)(2,1)}, bf16[64,16,128]{2,1,0:T(8,128)(2,1)S(1)}, u32[]{:S(2)}, u32[]{:S(2)}) collective-permute-start(bf16[64,16,128]{2,1,0:T(8,128)(2,1)} %param.25), channel_id=1, source_target_pairs={{32,0},{64,32},{96,64},{128,96},{160,128},{192,160},{224,192},{33,... | collective-permute-start | bytes 786440 | tf_op jit(solution)/shard_map/ppermute | solution.py:33
  8.2 9.9 %collective-permute-start = (bf16[64,1,128]{2,1,0:T(2,128)(2,1)S(1)}, bf16[64,1,128]{2,1,0:T(2,128)(2,1)S(1)}, u32[]{:S(2)}, u32[]{:S(2)}) collective-permute-start(bf16[64,1,128]{2,1,0:T(2,128)(2,1)S(1)} %get-tuple-element.145), channel_id=1, source_target_pairs={{0,32},{32,64},{64,96},{96,128},{128,160},{160,192},{192,224},{1,3... | collective-permute-start | bytes 49160 | tf_op jit(solution)/shard_map/ppermute | solution.py:30
  11.8 6.3 collective-permute-start.1
  18.1 1.2 copy-start.5
  18.1 1.2 copy-start.7
  45.0 63.4 %copy-start = (bf16[64,16,128]{2,1,0:T(8,128)(2,1)S(1)}, bf16[64,16,128]{2,1,0:T(8,128)(2,1)}, u32[]{:S(2)}) copy-start(bf16[64,16,128]{2,1,0:T(8,128)(2,1)} %param.24) | copy-start | bytes 786436
  45.0 79.4 %collective-permute-start.6 = (bf16[96,4096]{1,0:T(8,128)(2,1)S(1)}, bf16[96,4096]{1,0:T(8,128)(2,1)}, u32[]{:S(2)}, u32[]{:S(2)}) collective-permute-start(bf16[96,4096]{1,0:T(8,128)(2,1)S(1)} %reshape.641), channel_id=1, source_target_pairs={{2,0},{3,1},{4,2},{5,3},{6,4},{7,5},{8,6},{9,7},{10,8},{11,9},{12,... | collective-permute-start | bytes 2359304 | tf_op jit(solution)/shard_map/ppermute | solution.py:41
  53.1 74.2 %collective-permute-start.7 = (bf16[96,4096]{1,0:T(8,128)(2,1)S(1)}, bf16[96,4096]{1,0:T(8,128)(2,1)}, u32[]{:S(2)}, u32[]{:S(2)}) collective-permute-start(bf16[96,4096]{1,0:T(8,128)(2,1)S(1)} %reshape.641), channel_id=1, source_target_pairs={{1,0},{2,1},{3,2},{4,3},{5,4},{6,5},{7,6},{8,7},{9,8},{10,9},{11,1... | collective-permute-start | bytes 2359304 | tf_op jit(solution)/shard_map/ppermute | solution.py:41
  53.9 76.2 %collective-permute-start.8 = (bf16[96,4096]{1,0:T(8,128)(2,1)S(1)}, bf16[96,4096]{1,0:T(8,128)(2,1)S(1)}, u32[]{:S(2)}, u32[]{:S(2)}) collective-permute-start(bf16[96,4096]{1,0:T(8,128)(2,1)S(1)} %reshape.641), channel_id=1, source_target_pairs={{31,0},{0,1},{1,2},{2,3},{3,4},{4,5},{5,6},{6,7},{7,8},{8,9},{9,10... | collective-permute-start | bytes 2359304 | tf_op jit(solution)/shard_map/ppermute | solution.py:41
  54.5 77.1 %collective-permute-start.9 = (bf16[96,4096]{1,0:T(8,128)(2,1)S(1)}, bf16[96,4096]{1,0:T(8,128)(2,1)S(1)}, u32[]{:S(2)}, u32[]{:S(2)}) collective-permute-start(bf16[96,4096]{1,0:T(8,128)(2,1)S(1)} %reshape.641), channel_id=1, source_target_pairs={{30,0},{31,1},{0,2},{1,3},{2,4},{3,5},{4,6},{5,7},{6,8},{7,9},{8,1... | collective-permute-start | bytes 2359304 | tf_op jit(solution)/shard_map/ppermute | solution.py:41
  55.4 51.5 %collective-permute-start.2 = (bf16[64,18,1]{2,1,0:T(8,128)(2,1)S(1)}, bf16[64,18,1]{2,1,0:T(8,128)(2,1)S(1)}, u32[]{:S(2)}, u32[]{:S(2)}) collective-permute-start(bf16[64,18,1]{2,1,0:T(8,128)(2,1)S(1)} %get-tuple-element.143), channel_id=1, source_target_pairs={{0,1},{1,2},{2,3},{3,4},{4,5},{5,6},{6,7},{7,8},{8,9},{9,10},{10,1... | collective-permute-start | bytes 6920 | tf_op jit(solution)/shard_map/ppermute | solution.py:30
  106.9 14.3 %collective-permute-start.3 = (bf16[64,18,1]{2,1,0:T(8,128)(2,1)S(1)}, bf16[64,18,1]{2,1,0:T(8,128)(2,1)}, u32[]{:S(2)}, u32[]{:S(2)}) collective-permute-start(bf16[64,18,1]{2,1,0:T(8,128)(2,1)S(1)} %get-tuple-element.144), channel_id=1, source_target_pairs={{1,0},{2,1},{3,2},{4,3},{5,4},{6,5},{7,6},{8,7},{9,8},{10,9},{11,1... | collective-permute-start | bytes 6920 | tf_op jit(solution)/shard_map/ppermute | solution.py:33
  115.8 5.4 copy-start.6
  115.8 5.4 copy-start.8
  123.0 0.7 copy-start.10
  131.6 0.9 copy-start.2
  131.6 1.0 copy-start.3
  131.6 1.1 copy-start.4
  131.6 1.1 copy-start.15
  131.6 1.1 copy-start.16
  131.6 1.1 copy-start.17
  131.6 1.1 copy-start.18
  131.6 1.1 copy-start.19
  132.4 0.9 copy-start.13
  132.4 0.9 copy-start.14
  133.1 0.7 copy-start.9
  133.1 0.7 copy-start.11
  133.2 0.7 copy-start.12
  133.6 1.0 copy-start.1
  133.6 1.0 copy-start.20
  133.6 1.0 copy-start.21
  148.3 5.6 collective-permute-start.10
  154.2 14.7 %collective-permute-start.11 = (f32[3,5,1]{1,2,0:T(1,128)S(1)}, f32[3,5,1]{1,2,0:T(1,128)S(1)}, u32[]{:S(2)}, u32[]{:S(2)}) collective-permute-start(f32[3,5,1]{1,2,0:T(1,128)S(1)} %squeeze.25), channel_id=1, source_target_pairs={{0,1},{1,2},{2,3},{3,4},{4,5},{5,6},{6,7},{7,8},{8,9},{9,10},{10,1... | collective-permute-start | bytes 188 | tf_op jit(solution)/shard_map/ppermute | solution.py:22
  169.4 6.4 collective-permute-start.12
  175.8 7.3 %collective-permute-start.13 = (f32[3,5,2,1]{3,2,1,0:T(2,128)S(1)}, f32[3,5,2,1]{3,2,1,0:T(2,128)S(1)}, u32[]{:S(2)}, u32[]{:S(2)}) collective-permute-start(f32[3,5,2,1]{3,2,1,0:T(2,128)S(1)} %fusion.47), channel_id=1, source_target_pairs={{1,0},{2,1},{3,2},{4,3},{5,4},{6,5},{7,6},{8,7},{9,8},{10,9},{11,1... | collective-permute-start | bytes 368 | tf_op jit(solution)/shard_map/ppermute | solution.py:22
  185.2 3.6 collective-permute-start.14
  189.1 4.8 collective-permute-start.15
  360.6 5.0 collective-permute-start.16
  365.6 4.5 collective-permute-start.17
  372.1 4.0 collective-permute-start.18
  376.4 3.2 collective-permute-start.19
  536.3 5.0 collective-permute-start.20
  541.3 4.5 collective-permute-start.21
  547.8 4.0 collective-permute-start.22
  552.1 6.3 collective-permute-start.23
where the time goes:
time: 640 us; the launch traced here: 638 us
  blocking collectives  392 us (61%)
  waiting for transfers between devices  76.1 us (12%)
  starting transfers between devices  73.2 us (11%)
  local copies, waits for them, and re-layouts  69.5 us (11%)
  other arithmetic  19 us (3%)
  between operations  8.49 us (1%)
    psum x3, blocking collectives, squared(): return lax.psum(jnp.sum(vector * vector), ('gx', 'gy'))  237 us
    psum x2, blocking collectives, body(): step_size = norm_now / lax.psum(jnp.sum(direction * curved), ('gx', 'gy'))  155 us
    ppermute x3, waiting for transfers between devices, padded_2(): lax.ppermute(lax.slice_in_dim(block, block.shape[dim] - width, None, axis...  49.3 us
    ppermute x14, starting transfers between devices, from_behind(): return lax.ppermute(array, axis, pairs)  47.9 us
    ppermute x14, waiting for transfers between devices, from_behind(): return lax.ppermute(array, axis, pairs)  26.7 us
    reshape x2, local copies, waits for them, and re-layouts, local_bricks(): image.reshape(depth_count, EDGE, width_count, EDGE, height_count, EDGE)  12.9 us
    convert_element_type x3, local copies, waits for them, and re-layouts, body(): mismatch_rows = reference_rows.astype(jnp.float32) - warped  12.8 us
  transfers between devices with their start and end apart: 24, of which 14 were waited for; matrix products, arithmetic and copies ran while one was open for 5% of the time, Pallas kernels for 0%

commit v1 on v0

v1 whole, which is shorter than its diff:
```python
import jax
import jax.numpy as jnp
from jax import lax
from jax.experimental import pallas as pl
from jax.experimental.pallas import tpu as pltpu
from jax.sharding import PartitionSpec as P

EDGE = 16
EZ = 4
EYD = 8
SPAN = 2
ROUTES = 2 * SPAN + 1
NEL = 32
CAP = 8
VOL = 4096
NZ = 64
NY = 128
LAMBDA = 0.05
MESH = pl.DeviceIdType.MESH
F32 = jnp.float32
BF16 = jnp.bfloat16
EXACT = lax.Precision.HIGHEST

N_TABLE, N_BLOCK, N_FACE_X, N_FACE_Y, N_PACK, N_STENCIL, N_RHS, N_VEC = 4, 2, 2, 2, 4, 3, 11, 8
A_TABLE = 0
A_BLOCK = A_TABLE + N_TABLE
A_FACE_X = A_BLOCK + N_BLOCK
A_FACE_Y = A_FACE_X + N_FACE_X
A_PACK = A_FACE_Y + N_FACE_Y
A_STENCIL = A_PACK + N_PACK
A_RHS = A_STENCIL + N_STENCIL
A_VEC = A_RHS + N_RHS
A_END = A_VEC + 2 * N_VEC

OTHER_ROUTES = (1, 3, 0, 4)
RHS_OFFSETS = [(dp, dq) for dp in (-1, 0, 1, 2) for dq in (-1, 0, 1) if (dp, dq) != (0, 0)]
VEC_OFFSETS = [(dp, dq) for dp in (-1, 0, 1) for dq in (-1, 0, 1) if (dp, dq) != (0, 0)]
PAIRS = ((0, 0), (1, 1), (2, 2), (0, 1), (0, 2), (1, 2))


def iota(shape, dim):
    return lax.broadcasted_iota(jnp.int32, shape, dim)


def flag(condition):
    return jnp.where(condition, jnp.float32(1.0), jnp.float32(0.0))


def rolled(value, shift, axis):
    size = value.shape[axis]
    shift = shift % size
    return value if shift == 0 else pltpu.roll(value, shift, axis)


def hats(position):
    upper = (position.astype(F32) + 0.5) / EDGE
    return 1.0 - upper, upper


def kernel(
    nx, ny, route, within, xshift, fractions, ref, dfm, inc, mis,
    xb, tsend, trecv, fxs, fxr, fys, fyr, pmat, pacc, psend, precv, qmat, grad, refp, xrow, ss, sx, sy, sxy,
    kk, rrow, rs, rr, vs, vr, gs, gr, hs, hr, ssem, rsem, gssem, grsem, hssem, hrsem,
):
    p, q = lax.axis_index("gx"), lax.axis_index("gy")

    def at(dp, dq):
        return (lax.rem(p + dp + 2 * nx, nx), lax.rem(q + dq + 2 * ny, ny))

    def copy(src, dst, send_sem, recv_sem, dp, dq):
        c = pltpu.make_async_remote_copy(
            src_ref=src, dst_ref=dst, send_sem=send_sem, recv_sem=recv_sem,
            device_id=at(dp, dq), device_id_type=MESH,
        )
        c.start()
        return c

    started = []

    def send(number, src, dst, dp, dq):
        c = copy(src, dst, ssem.at[number], rsem.at[number], dp, dq)
        started.append(c)
        return c

    barrier = pltpu.get_barrier_semaphore()
    signals = 0
    for k in range(1, nx):
        pl.semaphore_signal(barrier, inc=1, device_id=at(k, 0), device_id_type=MESH)
        signals += 1
    for k in range(1, ny):
        pl.semaphore_signal(barrier, inc=1, device_id=at(0, k), device_id_type=MESH)
        signals += 1
    for dp in (-2, -1, 1, 2):
        for dq in (-1, 1):
            pl.semaphore_signal(barrier, inc=1, device_id=at(dp, dq), device_id_type=MESH)
            signals += 1

    lane, sub = iota((8, NY), 1), iota((8, NY), 0)
    block, inner = lane >> 4, lane & 15

    routes = [route[0, 0, e, 0] for e in range(NEL)]
    wanted = jnp.full((8, NY), -1, jnp.int32)
    count = jnp.zeros((8, NY), jnp.int32)
    for e in range(NEL):
        source = jnp.clip(p + xshift[0, 0, e] - 1, 0, nx - 1) - p + 1
        code = ((source * EZ + e // EYD) * EYD + within[0, 0, e]) * EDGE
        hit = sub == routes[e]
        wanted = jnp.where(hit & (count == block), inner + code, wanted)
        count = count + jnp.where(hit, 1, 0)
    tsend[...] = wanted
    pl.semaphore_wait(barrier, signals)
    tables = [
        send(A_TABLE + k, tsend, trecv.at[k], 0, r - SPAN) for k, r in enumerate(OTHER_ROUTES)
    ]
    blocks = [send(A_BLOCK, dfm, xb.at[1], -1, 0), send(A_BLOCK + 1, dfm, xb.at[0], 1, 0)]

    refp[0] = jnp.zeros((32, NY), F32)
    refp[NZ + 1] = jnp.zeros((32, NY), F32)
    refp[1 : NZ + 1, 8:24, :] = ref[...].astype(F32)
    fxs[0] = refp[1 : NZ + 1, 8, :].astype(BF16)
    fxs[1] = refp[1 : NZ + 1, 23, :].astype(BF16)
    faces_x = [
        send(A_FACE_X, fxs.at[0], fxr.at[1], -1, 0),
        send(A_FACE_X + 1, fxs.at[1], fxr.at[0], 1, 0),
    ]
    rows16, lanes16 = iota((16, NY), 0), iota((16, NY), 1)
    pick = ((rows16 == 0) & (lanes16 == 0)) | ((rows16 == 1) & (lanes16 == NY - 1))
    fys[...] = lax.dot_general(
        jnp.where(pick, 1.0, 0.0).astype(BF16), ref[...].reshape(NZ * EDGE, NY),
        (((1,), (1,)), ((), ())), preferred_element_type=F32,
    ).astype(BF16)
    faces_y = [
        send(A_FACE_Y, fys, fyr.at[1], 0, -1),
        send(A_FACE_Y + 1, fys, fyr.at[0], 0, 1),
    ]

    element = sub * EYD + block
    own_route = jnp.zeros((8, NY), jnp.int32)
    parts = [jnp.zeros((8, NY), jnp.int32) for _ in range(3)]
    for e in range(NEL):
        here = element == e
        own_route = jnp.where(here, routes[e], own_route)
        parts = [jnp.where(here, fractions[0, 0, e, c], parts[c]) for c in range(3)]
    slot = jnp.zeros((8, NY), jnp.int32)
    for e in range(NEL):
        slot = slot + jnp.where((element > e) & (own_route == routes[e]), 1, 0)
    first = (own_route * CAP + slot) * EDGE
    portion = [part.astype(F32) / EDGE for part in parts]
    target0 = first + inner
    target1 = first + jnp.minimum(inner + 1, EDGE - 1)

    for c in tables:
        c.wait_recv()
    asked = []
    for r in range(ROUTES):
        if r == SPAN:
            asked.append(wanted[r : r + 1])
        else:
            k = OTHER_ROUTES.index(r)
            asked.append(trecv[k, r : r + 1, :])
    asked = jnp.concatenate(asked, axis=1)

    def fill_pack(b, _):
        row = b * NY + iota((NY, ROUTES * NY), 0)
        pmat[pl.ds(pl.multiple_of(b * NY, NY), NY), :] = jnp.where(row == asked, 1.0, 0.0).astype(BF16)
        return 0

    lax.fori_loop(0, 3 * EZ, fill_pack, 0)

    def brick_rows(source):
        return jnp.concatenate(
            [source[z * EDGE : (z + 1) * EDGE].reshape(EDGE * EDGE, NY) for z in range(EZ)], axis=1
        )

    width = EZ * NY
    pacc[...] = jnp.dot(brick_rows(dfm), pmat[width : 2 * width, :], preferred_element_type=F32)
    blocks[1].wait_recv()
    pacc[...] += jnp.dot(brick_rows(xb[0]), pmat[0:width, :], preferred_element_type=F32)
    blocks[0].wait_recv()
    pacc[...] += jnp.dot(brick_rows(xb[1]), pmat[2 * width : 3 * width, :], preferred_element_type=F32)
    packs = []
    for k, r in enumerate(OTHER_ROUTES):
        psend[k] = pacc[:, r * NY : (r + 1) * NY].astype(BF16)
        packs.append(send(A_PACK + k, psend.at[k], precv.at[r], 0, SPAN - r))
    precv[SPAN] = pacc[:, SPAN * NY : (SPAN + 1) * NY].astype(BF16)

    for c in faces_x + faces_y:
        c.wait_recv()
    refp[1 : NZ + 1, 7, :] = fxr[0].astype(F32) * flag(p > 0)
    refp[1 : NZ + 1, 24, :] = fxr[1].astype(F32) * flag(p < nx - 1)
    here, there = iota((NY, NY), 1), iota((NY, NY), 0)
    differ = jnp.where(there == here + 1, 0.5, jnp.where(there == here - 1, -0.5, 0.0)).astype(BF16)
    rows32, lanes32 = iota((32, NY), 0), iota((32, NY), 1)
    ends = jnp.where(
        (rows32 == 1) & (lanes32 == 0), flag(q > 0) * -0.5,
        jnp.where((rows32 == 16) & (lanes32 == NY - 1), flag(q < ny - 1) * 0.5, 0.0),
    ).astype(BF16)
    sides = jnp.concatenate([fyr[0], fyr[1]], axis=0)
    along_y = jnp.dot(ref[...].reshape(NZ * EDGE, NY), differ, preferred_element_type=F32)
    along_y = along_y + lax.dot_general(sides, ends, (((0,), (0,)), ((), ())), preferred_element_type=F32)
    grad[2] = along_y.astype(BF16).reshape(NZ, EDGE, NY)

    def slope(b, _):
        base = b * 4
        below, above = refp[pl.ds(base, 4), 8:24, :], refp[pl.ds(base + 2, 4), 8:24, :]
        grad[0, pl.ds(base, 4)] = ((above - below) * 0.5).astype(BF16)
        left, right = refp[pl.ds(base + 1, 4), 7:23, :], refp[pl.ds(base + 1, 4), 9:25, :]
        grad[1, pl.ds(base, 4)] = ((right - left) * 0.5).astype(BF16)
        return 0

    lax.fori_loop(0, NZ // 4, slope, 0)

    rowm, colm = iota((24, 96), 0), iota((24, 96), 1)
    low_x, high_x = hats(colm & 15)
    order = rowm >> 3
    weight_x = jnp.where(order == 0, low_x * low_x, jnp.where(order == 1, low_x * high_x, high_x * high_x))
    weight_x = jnp.where((rowm & 7) == (colm >> 4), weight_x, 0.0)

    def moments(z, _):
        total = [[None] * 6 for _ in range(3)]
        for i in range(EDGE):
            g = [grad[c, z * EDGE + i].astype(F32) for c in range(3)]
            high = (i + 0.5) / EDGE
            low = 1.0 - high
            for k, (a, b) in enumerate(PAIRS):
                product = g[a] * g[b]
                for m, weight in enumerate((low * low, low * high, high * high)):
                    term = product * weight
                    total[m][k] = term if i == 0 else total[m][k] + term
        for m in range(3):
            rows = jnp.dot(weight_x, jnp.concatenate(total[m], axis=0), precision=EXACT, preferred_element_type=F32)
            xrow[pl.ds(pl.multiple_of((z * 3 + m) * 24, 24), 24), :] = rows
        return 0

    lax.fori_loop(0, EZ, moments, 0)
    fine, coarse = iota((NY, 3 * NY), 0), iota((NY, 3 * NY), 1)
    low_y, high_y = hats(fine & 15)
    row_y, node_y, step_y = fine >> 4, (coarse & 15) - 4, (coarse >> 7) - 1
    starts, closes = row_y == node_y, row_y + 1 == node_y
    mixed = low_y * high_y
    weight_y = jnp.where(
        step_y == 1, jnp.where(starts, mixed, 0.0),
        jnp.where(
            step_y == -1, jnp.where(closes, mixed, 0.0),
            jnp.where(starts, low_y * low_y, 0.0) + jnp.where(closes, high_y * high_y, 0.0),
        ),
    ) * (1.0 / VOL)
    yrow = jnp.dot(xrow[...], weight_y, precision=EXACT, preferred_element_type=F32)
    on = [block == z for z in range(EZ + 1)]
    for m in range(3):
        for dy in range(3):
            def term(z, depth):
                start = (z * 3 + depth) * 24 + m * 8
                return yrow[start : start + 8, dy * NY : (dy + 1) * NY]

            zero = jnp.zeros((8, NY), F32)
            down, same, up = zero, zero, zero
            for z in range(EZ):
                cross = term(z, 1)
                up = jnp.where(on[z], cross, up)
                down = jnp.where(on[z + 1], cross, down)
                same = same + jnp.where(on[z], term(z, 0), 0.0) + jnp.where(on[z + 1], term(z, 2), 0.0)
            ss[m, dy], ss[m, 3 + dy], ss[m, 6 + dy] = down, same, up
    stencils = [
        send(A_STENCIL, ss.at[1:3], sx, 1, 0),
        send(A_STENCIL + 1, ss, sy, 0, 1),
        send(A_STENCIL + 2, ss.at[1:3], sxy, 1, 1),
    ]

    for z in range(EZ):
        def fill_place(b, _):
            row = b * NY + iota((NY, NY), 0)
            high = portion[2][z : z + 1]
            place = jnp.where(row == target0[z : z + 1], 1.0 - high, 0.0)
            place = place + jnp.where(row == target1[z : z + 1], high, 0.0)
            qmat[pl.ds(pl.multiple_of(b * NY, NY), NY), z * NY : (z + 1) * NY] = place.astype(BF16)
            return 0

        lax.fori_loop(0, ROUTES, fill_place, 0)

    column = inner - 4
    own = (column >= 0) & (column < EYD) & (block <= EZ)
    has_x, has_y = flag(p > 0), flag(q > 0)
    for c in stencils:
        c.wait_recv()

    def fold(from_y):
        return jnp.where(inner < 8, rolled(from_y, -8, 1), 0.0) * has_y

    for t in range(9):
        here0 = ss[0, t] + fold(sy[0, t])
        here1 = ss[1, t] + fold(sy[1, t])
        back1 = (sx[0, t] + fold(sxy[0, t])) * has_x
        back2 = (sx[1, t] + fold(sxy[1, t])) * has_x
        kk[0, t] = jnp.where(own, back1, 0.0)
        kk[1, t] = jnp.where(own, here0 + back2, 0.0)
        kk[2, t] = jnp.where(own, here1, 0.0)

    for c in packs:
        c.wait_recv()
    taken = jnp.concatenate([precv[r] for r in range(ROUTES)], axis=1)
    fetched = jnp.dot(taken, qmat[...], preferred_element_type=F32)
    row8, col16 = iota((8, EDGE), 0), iota((8, EDGE), 1)
    low_j, high_j = hats(iota((EDGE, 1), 0))
    for z in range(EZ):
        voxels = fetched[:, z * NY : (z + 1) * NY].reshape(EDGE, EDGE, NY)
        high = portion[1][z : z + 1].reshape(1, 1, NY)
        ahead = jnp.concatenate([voxels[:, 1:], voxels[:, EDGE - 1 :]], axis=1)
        voxels = (1.0 - high) * voxels + high * ahead
        high = portion[0][z : z + 1].reshape(1, 1, NY)
        ahead = jnp.concatenate([voxels[1:], voxels[EDGE - 1 :]], axis=0)
        voxels = (1.0 - high) * voxels + high * ahead
        left = refp[1 + z * EDGE : 1 + (z + 1) * EDGE, 8:24, :] - voxels
        mis[z * EDGE : (z + 1) * EDGE] = left
        sums = [[None] * 3 for _ in range(2)]
        for i in range(EDGE):
            high = (i + 0.5) / EDGE
            for c in range(3):
                value = grad[c, z * EDGE + i].astype(F32) * left[i]
                for m, weight in enumerate((1.0 - high, high)):
                    sums[m][c] = value * weight if i == 0 else sums[m][c] + value * weight
        for m in range(2):
            rows = [jnp.sum(sums[m][c] * w, axis=0, keepdims=True) for w in (low_j, high_j) for c in range(3)]
            blank = jnp.zeros((1, NY), F32)
            start = (z * 2 + m) * 8
            rrow[start : start + 8, :] = jnp.concatenate(rows[:3] + [blank] + rows[3:] + [blank], axis=0)
    fine, coarse = iota((NY, NY), 0), iota((NY, NY), 1)
    low_y, high_y = hats(fine & 15)
    row_y, node_y = fine >> 4, (coarse & 15) - 4
    weight_y = (
        jnp.where(row_y == node_y, low_y, 0.0) + jnp.where(row_y + 1 == node_y, high_y, 0.0)
    ) * (1.0 / VOL)
    nodes = jnp.dot(rrow[...], weight_y, precision=EXACT, preferred_element_type=F32)
    tile = jnp.zeros((8, NY), F32)
    for z in range(EZ):
        for m in range(2):
            start = (z * 2 + m) * 8
            tile = tile + jnp.where(on[z + m], nodes[start : start + 8], 0.0)
    rs[...] = tile

    def gathered(mine, arrived, dp):
        total = mine
        for dq, shift, keep in ((1, 8, inner >= 8), (-1, -8, inner < 8)):
            inside = flag((q + dq >= 0) & (q + dq < ny))
            total = total + jnp.where(keep, rolled(arrived(dp, dq), shift, 1), 0.0) * inside
        return total * flag((p + dp >= 0) & (p + dp < nx))

    sent = [send(A_RHS + k, rs, rr.at[k], -dp, -dq) for k, (dp, dq) in enumerate(
        [(-dp, -dq) for dp, dq in RHS_OFFSETS])]
    for c in sent:
        c.wait_recv()

    def rhs_from(dp, dq):
        return rs[...] if (dp, dq) == (0, 0) else rr[RHS_OFFSETS.index((-dp, -dq))]

    around = {dp: gathered(rhs_from(dp, 0), rhs_from, dp) for dp in (-2, -1, 0, 1)}
    first3 = sub < 3
    inside_y = q * EYD + column < ny * EYD
    vector = []
    for dp in (-1, 0, 1):
        whole = around[dp] + rolled(around[dp - 1], 4, 0)
        vector.append(jnp.where(first3 & inside_y, whole, 0.0) * flag((p + dp >= 0) & (p + dp < nx)))

    def apply(vector):
        straight, crossed = jnp.zeros((8, NY), F32), jnp.zeros((8, NY), F32)
        for dx in range(3):
            u = [vector[dx][c : c + 1] for c in range(3)]
            second = jnp.where(sub == 0, u[0], jnp.where((sub == 1) | (sub == 3), u[1], u[2]))
            third = jnp.where(sub == 5, u[1], u[0])
            for t in range(9):
                shift = -((t // 3 - 1) * 16 + t % 3 - 1)
                weight = kk[dx, t]
                straight = straight + weight * rolled(second, shift, 1)
                crossed = crossed + weight * rolled(third, shift, 1)
        s = [straight[k : k + 1] for k in range(6)]
        out = [
            s[0] + s[3] + s[4],
            s[1] + s[5] + crossed[3:4],
            s[2] + crossed[4:5] + crossed[5:6],
        ]
        image = jnp.where(sub == 0, out[0], jnp.where(sub == 1, out[1], out[2]))
        return jnp.where(own & first3, image + LAMBDA * vector[1], 0.0)

    powers = [jnp.where(own, vector[1], 0.0)]
    for step in range(3):
        image = apply(vector)
        powers.append(image)
        if step < 2:
            vs[step] = image
            sent = [
                send(A_VEC + step * N_VEC + k, vs.at[step], vr.at[step, k], dp, dq)
                for k, (dp, dq) in enumerate(VEC_OFFSETS)
            ]
            for c in sent:
                c.wait_recv()

            def arrived(dp, dq):
                return vr[step, VEC_OFFSETS.index((-dp, -dq))]

            vector = [gathered(image if dp == 0 else arrived(dp, 0), arrived, dp) for dp in (-1, 0, 1)]

    tile = jnp.zeros((8, NY), F32)
    for k in range(6):
        product = jnp.sum(powers[k // 2] * powers[(k + 1) // 2], axis=0, keepdims=True)
        tile = jnp.where(sub == k, product, tile)
    gs[...] = tile

    def to_x(k, _):
        copy(gs, gr.at[k - 1], gssem.at[k - 1], grsem.at[k - 1], k, 0)
        return 0

    def from_x(k, total):
        pltpu.make_async_remote_copy(
            src_ref=gs, dst_ref=gr.at[k - 1], send_sem=gssem.at[k - 1], recv_sem=grsem.at[k - 1],
            device_id=at(k, 0), device_id_type=MESH,
        ).wait()
        return total + gr[k - 1]

    lax.fori_loop(1, nx, to_x, 0)
    tile = lax.fori_loop(1, nx, from_x, tile)
    hs[...] = tile

    def to_y(k, _):
        copy(hs, hr.at[k - 1], hssem.at[k - 1], hrsem.at[k - 1], 0, k)
        return 0

    def from_y(k, total):
        pltpu.make_async_remote_copy(
            src_ref=hs, dst_ref=hr.at[k - 1], send_sem=hssem.at[k - 1], recv_sem=hrsem.at[k - 1],
            device_id=at(0, k), device_id_type=MESH,
        ).wait()
        return total + hr[k - 1]

    lax.fori_loop(1, ny, to_y, 0)
    tile = lax.fori_loop(1, ny, from_y, tile)
    total = jnp.broadcast_to(jnp.sum(tile, axis=1, keepdims=True), (8, NY))
    moment = [total[k : k + 1] for k in range(6)]

    def product(a, b, more):
        value = 0.0
        for i, left in enumerate(a):
            for j, right in enumerate(b):
                value = value + left * right * moment[i + j + more]
        return value

    blank, unit = jnp.zeros((1, NY), F32), jnp.ones((1, NY), F32)
    answer, residual, direction = [blank] * 3, [unit], [unit]
    norm = moment[0]
    for step in range(3):
        bend = product(direction, direction, 1)
        alpha = norm / bend
        answer = [answer[i] + alpha * direction[i] if i < len(direction) else answer[i] for i in range(3)]
        if step < 2:
            grown = residual + [blank]
            residual = [
                grown[i] - alpha * direction[i - 1] if i > 0 else grown[i] for i in range(step + 2)
            ]
            after = product(residual, residual, 0)
            beta = after / norm
            norm = after
            widened = direction + [blank]
            direction = [residual[i] + beta * widened[i] for i in range(step + 2)]
    inc[...] = answer[0] * powers[0] + answer[1] * powers[1] + answer[2] * powers[2]
    for c in started:
        c.wait_send()


def body(nx, ny, reference_image, deformed_image, route, within, xshift, fractions):
    vmem = pl.BlockSpec(memory_space=pltpu.VMEM)
    smem = pl.BlockSpec(memory_space=pltpu.SMEM)
    half = (NZ, EDGE, NY)
    tile = (8, NY)
    inc, mis = pl.pallas_call(
        lambda *refs: kernel(nx, ny, *refs),
        name="correlate",
        out_shape=(jax.ShapeDtypeStruct(tile, F32), jax.ShapeDtypeStruct(half, F32)),
        in_specs=[smem] * 4 + [vmem] * 2,
        out_specs=(vmem, vmem),
        scratch_shapes=[
            pltpu.VMEM((2,) + half, BF16),
            pltpu.VMEM(tile, jnp.int32),
            pltpu.VMEM((4,) + tile, jnp.int32),
            pltpu.VMEM((2, NZ, NY), BF16),
            pltpu.VMEM((2, NZ, NY), BF16),
            pltpu.VMEM((16, NZ * EDGE), BF16),
            pltpu.VMEM((2, 16, NZ * EDGE), BF16),
            pltpu.VMEM((3 * EZ * NY, ROUTES * NY), BF16),
            pltpu.VMEM((EDGE * EDGE, ROUTES * NY), F32),
            pltpu.VMEM((4, EDGE * EDGE, NY), BF16),
            pltpu.VMEM((ROUTES, EDGE * EDGE, NY), BF16),
            pltpu.VMEM((ROUTES * NY, EZ * NY), BF16),
            pltpu.VMEM((3,) + half, BF16),
            pltpu.VMEM((NZ + 2, 32, NY), F32),
            pltpu.VMEM((12 * 24, NY), F32),
            pltpu.VMEM((3, 9) + tile, F32),
            pltpu.VMEM((2, 9) + tile, F32),
            pltpu.VMEM((3, 9) + tile, F32),
            pltpu.VMEM((2, 9) + tile, F32),
            pltpu.VMEM((3, 9) + tile, F32),
            pltpu.VMEM((64, NY), F32),
            pltpu.VMEM(tile, F32),
            pltpu.VMEM((N_RHS,) + tile, F32),
            pltpu.VMEM((2,) + tile, F32),
            pltpu.VMEM((2, N_VEC) + tile, F32),
            pltpu.VMEM(tile, F32),
            pltpu.VMEM((nx - 1,) + tile, F32),
            pltpu.VMEM(tile, F32),
            pltpu.VMEM((ny - 1,) + tile, F32),
            pltpu.SemaphoreType.DMA((A_END,)),
            pltpu.SemaphoreType.DMA((A_END,)),
            pltpu.SemaphoreType.DMA((nx - 1,)),
            pltpu.SemaphoreType.DMA((nx - 1,)),
            pltpu.SemaphoreType.DMA((ny - 1,)),
            pltpu.SemaphoreType.DMA((ny - 1,)),
        ],
        compiler_params=pltpu.CompilerParams(
            collective_id=0, has_side_effects=True, vmem_limit_bytes=48 << 20
        ),
    )(route, within, xshift, fractions, reference_image, deformed_image)
    grid = inc[:3].reshape(3, 8, 16)
    return grid[:, : EZ + 1, None, 4 : 4 + EYD], mis


def solution(mesh):
    nx, ny = mesh.shape["gx"], mesh.shape["gy"]
    placed = (
        P(None, "gx", "gy"),
        P(None, "gx", "gy"),
        P("gx", "gy", None, None),
        P("gx", "gy", None),
        P("gx", "gy", None),
        P("gx", "gy", None, None),
    )
    return jax.shard_map(
        lambda *blocks: body(nx, ny, *blocks),
        mesh=mesh,
        in_specs=placed,
        out_specs=(P(None, None, "gx", "gy"), P(None, "gx", "gy")),
        check_vma=False,
    )
```

time: 640 us -> 61.7 us (0.10)
  blocking collectives: 392 us -> 0 us
  waiting for transfers between devices: 76.1 us -> 0 us
  starting transfers between devices: 73.2 us -> 0 us
  local copies, waits for them, and re-layouts: 69.5 us -> 4.88 us
  Pallas kernels: 0 us -> 55.9 us
  other arithmetic: 19 us -> 0 us
  between operations: 8.49 us -> 0.66 us
    psum x5 -> x0, blocking collectives: 392 us -> none  [the longest x3 237 us: squared(): return lax.psum(jnp.sum(vector * vector), ('gx', 'gy'))]
    ppermute x24 -> x0, waiting for transfers between devices: 76.1 us -> none  [the longest x3 49.3 us: padded_2(): lax.ppermute(lax.slice_in_dim(block, block.shape[dim] - width, None, axis...]
    ppermute x24 -> x0, starting transfers between devices: 73.2 us -> none  [the longest x14 47.9 us: from_behind(): return lax.ppermute(array, axis, pairs)]
    pallas_call x0 -> x1, Pallas kernels: none -> 55.9 us  [body(): pl.pallas_call(lambda *refs: kernel(nx, ny, *refs), name='correlate', out...]
    reshape x10 -> x1, local copies, waits for them, and re-layouts: 38.3 us -> 0.08 us  [body(): grid = inc[:3].reshape(3, 8, 16)]
    convert_element_type x3 -> x0, local copies, waits for them, and re-layouts: 12.8 us -> none  [body(): mismatch_rows = reference_rows.astype(jnp.float32) - warped]
    gather x5 -> x0, local copies, waits for them, and re-layouts: 8.59 us -> none  [the longest x4 7.88 us: body(): picked = jnp.take(window, source_index, axis=0)]
    reduce_sum x20 -> x0, other arithmetic: 6.74 us -> none  [the longest x3 1.87 us: body(): step_size = norm_now / lax.psum(jnp.sum(direction * curved), ('gx', 'gy'))]
  transfers between devices with their start and end apart: 24 -> 0, of which waited for: 14 -> 0; matrix products, arithmetic and copies ran while one was open for 5% -> 0% of each run, Pallas kernels for 0% -> 0%
where the time goes in v1:
time: 61.7 us; the launch traced here: 61.5 us
  Pallas kernels  55.9 us (91%)
  local copies, waits for them, and re-layouts  4.88 us (8%)
  between operations  0.66 us (1%)
    pallas_call x1, Pallas kernels, body(): pl.pallas_call(lambda *refs: kernel(nx, ny, *refs), name='correlate', out...  55.9 us
    unnamed x15, local copies, waits for them, and re-layouts  4.72 us

profile of v1, /device:TPU:1, one launch (start us, length us, event | category | flops | bytes accessed | tf_op | source)
XLA Modules:
  0.0 61.5 jit_solution(14607932018199231705)
XLA Ops:
  0.6 0.0 copy-start.4
  0.6 0.7 %copy.8.refs_0_ = s32[1,1,32,1]{3,2,1,0:T(8,128)S(1)} copy(s32[1,1,32,1]{2,3,1,0:T(1,128)} %param.8) | data formatting | bytes 256 | tf_op args[2]
  1.4 0.0 copy-done.4
  1.4 0.0 copy-start.2
  1.4 0.0 copy-start.3
  1.4 0.1 copy.9.refs_3_
  1.5 0.6 copy-done.2
  2.0 0.0 copy-done.3
  2.1 0.0 copy-start
  2.1 0.9 %copy-done = bf16[64,16,128]{2,1,0:T(8,128)(2,1)S(1)} copy-done((bf16[64,16,128]{2,1,0:T(8,128)(2,1)S(1)}, bf16[64,16,128]{2,1,0:T(8,128)(2,1)}, u32[]{:S(2)}) %copy-start) | copy-done | bytes 262168
  3.0 0.0 copy-start.1
  3.0 0.9 %copy-done.1 = bf16[64,16,128]{2,1,0:T(8,128)(2,1)S(1)} copy-done((bf16[64,16,128]{2,1,0:T(8,128)(2,1)S(1)}, bf16[64,16,128]{2,1,0:T(8,128)(2,1)}, u32[]{:S(2)}) %copy-start.1) | copy-done | bytes 262168
  4.0 55.9 %correlate.1 = (f32[8,128]{1,0:T(8,128)S(1)}, f32[64,16,128]{2,1,0:T(8,128)S(1)}) custom-call(s32[1,1,32,1]{3,2,1,0:T(8,128)S(1)} %copy.8.refs_0_, s32[1,1,32]{2,1,0:T(1,128)S(1)} %copy-done.2, s32[1,1,32]{2,1,0:T(1,128)S(1)} %copy-done.3, s32[1,1,32,3]{3,2,1,0:T(8,128)S(1)} %copy.9.refs_3_, bf16[64,16,128]{2,1,0:T(8,128)(2,1)S(1)} %copy-done, ...), custom_call_target="tpu_custom_call" | custom-call | tf_op jit(solution)/shard_map/correlate/pallas_call | solution.py:473
  59.9 0.1 reshape.7
  60.0 0.1 slice.8
  60.1 0.6 copy.11
  60.7 0.8 %copy.16 = f32[64,16,128]{2,1,0:T(8,128)} copy(f32[64,16,128]{2,1,0:T(8,128)S(1)} %get-tuple-element.11) | data formatting | bytes 1048576
  (2 shorter events, 0.0 us)
Async XLA Ops:
  0.6 0.8 %copy-start.4 = (s32[1,1,32,3]{2,1,3,0:T(1,128)S(1)}, s32[1,1,32,3]{2,1,3,0:T(1,128)}, u32[]{:S(2)}) copy-start(s32[1,1,32,3]{2,1,3,0:T(1,128)} %param.11) | copy-start | bytes 1156
  1.4 0.7 %copy-start.2 = (s32[1,1,32]{2,1,0:T(1,128)S(1)}, s32[1,1,32]{2,1,0:T(1,128)}, u32[]{:S(2)}) copy-start(s32[1,1,32]{2,1,0:T(1,128)} %refs_1_.1) | copy-start | bytes 388
  1.4 0.7 %copy-start.3 = (s32[1,1,32]{2,1,0:T(1,128)S(1)}, s32[1,1,32]{2,1,0:T(1,128)}, u32[]{:S(2)}) copy-start(s32[1,1,32]{2,1,0:T(1,128)} %refs_2_.1) | copy-start | bytes 388
  2.1 0.9 %copy-start = (bf16[64,16,128]{2,1,0:T(8,128)(2,1)S(1)}, bf16[64,16,128]{2,1,0:T(8,128)(2,1)}, u32[]{:S(2)}) copy-start(bf16[64,16,128]{2,1,0:T(8,128)(2,1)} %refs_4_.1) | copy-start | bytes 786436
  3.0 0.9 %copy-start.1 = (bf16[64,16,128]{2,1,0:T(8,128)(2,1)S(1)}, bf16[64,16,128]{2,1,0:T(8,128)(2,1)}, u32[]{:S(2)}) copy-start(bf16[64,16,128]{2,1,0:T(8,128)(2,1)} %refs_5_.1) | copy-start | bytes 786436

commit v2 on v1

--- a/solution.py
+++ b/solution.py
@@ -52,13 +52,25 @@
     return value if shift == 0 else pltpu.roll(value, shift, axis)
 
 
+def halves(value):
+    high = value.astype(BF16)
+    return high, (value - high.astype(F32)).astype(BF16)
+
+
+def near_exact(left, right):
+    a, b = halves(left), halves(right)
+    total = jnp.dot(a[0], b[1], preferred_element_type=F32) + jnp.dot(a[1], b[0], preferred_element_type=F32)
+    return total + jnp.dot(a[0], b[0], preferred_element_type=F32)
+
+
 def hats(position):
     upper = (position.astype(F32) + 0.5) / EDGE
     return 1.0 - upper, upper
 
 
 def kernel(
-    nx, ny, route, within, xshift, fractions, ref, dfm, inc, mis,
+    nx, ny, route_hbm, within_hbm, xshift_hbm, fractions_hbm, ref_hbm, dfm_hbm, inc, mis,
+    route, within, xshift, fractions, ref, dfm, lsem, gossip,
     xb, tsend, trecv, fxs, fxr, fys, fyr, pmat, pacc, psend, precv, qmat, grad, refp, xrow, ss, sx, sy, sxy,
     kk, rrow, rs, rr, vs, vr, gs, gr, hs, hr, ssem, rsem, gssem, grsem, hssem, hrsem,
 ):
@@ -82,23 +94,34 @@
         started.append(c)
         return c
 
+    near = ((1, 0), (-1, 0), (0, 1), (0, -1), (0, 2), (0, -2))
     barrier = pltpu.get_barrier_semaphore()
-    signals = 0
-    for k in range(1, nx):
-        pl.semaphore_signal(barrier, inc=1, device_id=at(k, 0), device_id_type=MESH)
-        signals += 1
-    for k in range(1, ny):
-        pl.semaphore_signal(barrier, inc=1, device_id=at(0, k), device_id_type=MESH)
-        signals += 1
-    for dp in (-2, -1, 1, 2):
-        for dq in (-1, 1):
-            pl.semaphore_signal(barrier, inc=1, device_id=at(dp, dq), device_id_type=MESH)
-            signals += 1
+    for dp, dq in near:
+        pl.semaphore_signal(barrier, inc=1, device_id=at(dp, dq), device_id_type=MESH)
+    loads = []
+    for k, (src, dst) in enumerate((
+        (route_hbm, route), (within_hbm, within), (xshift_hbm, xshift), (fractions_hbm, fractions),
+        (ref_hbm, ref), (dfm_hbm, dfm),
+    )):
+        loads.append(pltpu.make_async_copy(src, dst, lsem.at[k]))
+        loads[k].start()
+
+    def tell(number, *places):
+        for dp, dq in places:
+            pl.semaphore_signal(gossip.at[number], inc=1, device_id=at(dp, dq), device_id_type=MESH)
+
+    def hear(number, count):
+        pl.semaphore_wait(gossip.at[number], count)
+
+    pl.semaphore_wait(barrier, len(near))
+    blocks = [send(A_BLOCK, dfm_hbm, xb.at[1], -1, 0), send(A_BLOCK + 1, dfm_hbm, xb.at[0], 1, 0)]
 
     lane, sub = iota((8, NY), 1), iota((8, NY), 0)
     block, inner = lane >> 4, lane & 15
 
-    routes = [route[0, 0, e, 0] for e in range(NEL)]
+    for c in loads[:3]:
+        c.wait()
+    routes = [route[0, 0, e] for e in range(NEL)]
     wanted = jnp.full((8, NY), -1, jnp.int32)
     count = jnp.zeros((8, NY), jnp.int32)
     for e in range(NEL):
@@ -108,12 +131,11 @@
         wanted = jnp.where(hit & (count == block), inner + code, wanted)
         count = count + jnp.where(hit, 1, 0)
     tsend[...] = wanted
-    pl.semaphore_wait(barrier, signals)
     tables = [
         send(A_TABLE + k, tsend, trecv.at[k], 0, r - SPAN) for k, r in enumerate(OTHER_ROUTES)
     ]
-    blocks = [send(A_BLOCK, dfm, xb.at[1], -1, 0), send(A_BLOCK + 1, dfm, xb.at[0], 1, 0)]
-
+
+    loads[4].wait()
     refp[0] = jnp.zeros((32, NY), F32)
     refp[NZ + 1] = jnp.zeros((32, NY), F32)
     refp[1 : NZ + 1, 8:24, :] = ref[...].astype(F32)
@@ -134,13 +156,14 @@
         send(A_FACE_Y + 1, fys, fyr.at[0], 0, 1),
     ]
 
+    loads[3].wait()
     element = sub * EYD + block
     own_route = jnp.zeros((8, NY), jnp.int32)
     parts = [jnp.zeros((8, NY), jnp.int32) for _ in range(3)]
     for e in range(NEL):
         here = element == e
         own_route = jnp.where(here, routes[e], own_route)
-        parts = [jnp.where(here, fractions[0, 0, e, c], parts[c]) for c in range(3)]
+        parts = [jnp.where(here, fractions[0, c, 0, e], parts[c]) for c in range(3)]
     slot = jnp.zeros((8, NY), jnp.int32)
     for e in range(NEL):
         slot = slot + jnp.where((element > e) & (own_route == routes[e]), 1, 0)
@@ -148,41 +171,6 @@
     portion = [part.astype(F32) / EDGE for part in parts]
     target0 = first + inner
     target1 = first + jnp.minimum(inner + 1, EDGE - 1)
-
-    for c in tables:
-        c.wait_recv()
-    asked = []
-    for r in range(ROUTES):
-        if r == SPAN:
-            asked.append(wanted[r : r + 1])
-        else:
-            k = OTHER_ROUTES.index(r)
-            asked.append(trecv[k, r : r + 1, :])
-    asked = jnp.concatenate(asked, axis=1)
-
-    def fill_pack(b, _):
-        row = b * NY + iota((NY, ROUTES * NY), 0)
-        pmat[pl.ds(pl.multiple_of(b * NY, NY), NY), :] = jnp.where(row == asked, 1.0, 0.0).astype(BF16)
-        return 0
-
-    lax.fori_loop(0, 3 * EZ, fill_pack, 0)
-
-    def brick_rows(source):
-        return jnp.concatenate(
-            [source[z * EDGE : (z + 1) * EDGE].reshape(EDGE * EDGE, NY) for z in range(EZ)], axis=1
-        )
-
-    width = EZ * NY
-    pacc[...] = jnp.dot(brick_rows(dfm), pmat[width : 2 * width, :], preferred_element_type=F32)
-    blocks[1].wait_recv()
-    pacc[...] += jnp.dot(brick_rows(xb[0]), pmat[0:width, :], preferred_element_type=F32)
-    blocks[0].wait_recv()
-    pacc[...] += jnp.dot(brick_rows(xb[1]), pmat[2 * width : 3 * width, :], preferred_element_type=F32)
-    packs = []
-    for k, r in enumerate(OTHER_ROUTES):
-        psend[k] = pacc[:, r * NY : (r + 1) * NY].astype(BF16)
-        packs.append(send(A_PACK + k, psend.at[k], precv.at[r], 0, SPAN - r))
-    precv[SPAN] = pacc[:, SPAN * NY : (SPAN + 1) * NY].astype(BF16)
 
     for c in faces_x + faces_y:
         c.wait_recv()
@@ -209,12 +197,66 @@
         return 0
 
     lax.fori_loop(0, NZ // 4, slope, 0)
+    tell(0, (1, 0), (-1, 0))
+
+    for z in range(EZ):
+        def fill_place(b, _):
+            row = b * NY + iota((NY, NY), 0)
+            high = portion[2][z : z + 1]
+            place = jnp.where(row == target0[z : z + 1], 1.0 - high, 0.0)
+            place = place + jnp.where(row == target1[z : z + 1], high, 0.0)
+            qmat[pl.ds(pl.multiple_of(b * NY, NY), NY), z * NY : (z + 1) * NY] = place.astype(BF16)
+            return 0
+
+        lax.fori_loop(0, ROUTES, fill_place, 0)
+
+    for c in tables:
+        c.wait_recv()
+    tell(2, (0, 4), (0, -4))
+    asked = []
+    for r in range(ROUTES):
+        if r == SPAN:
+            asked.append(wanted[r : r + 1])
+        else:
+            k = OTHER_ROUTES.index(r)
+            asked.append(trecv[k, r : r + 1, :])
+    asked = jnp.concatenate(asked, axis=1)
+
+    def fill_pack(b, _):
+        row = b * NY + iota((NY, ROUTES * NY), 0)
+        pmat[pl.ds(pl.multiple_of(b * NY, NY), NY), :] = jnp.where(row == asked, 1.0, 0.0).astype(BF16)
+        return 0
+
+    lax.fori_loop(0, 3 * EZ, fill_pack, 0)
+
+    def brick_rows(source):
+        return jnp.concatenate(
+            [source[z * EDGE : (z + 1) * EDGE].reshape(EDGE * EDGE, NY) for z in range(EZ)], axis=1
+        )
+
+    width = EZ * NY
+    loads[5].wait()
+    pacc[...] = jnp.dot(brick_rows(dfm), pmat[width : 2 * width, :], preferred_element_type=F32)
+    blocks[1].wait_recv()
+    pacc[...] += jnp.dot(brick_rows(xb[0]), pmat[0:width, :], preferred_element_type=F32)
+    blocks[0].wait_recv()
+    pacc[...] += jnp.dot(brick_rows(xb[1]), pmat[2 * width : 3 * width, :], preferred_element_type=F32)
+    packs = []
+    for k, r in enumerate(OTHER_ROUTES):
+        psend[k] = pacc[:, r * NY : (r + 1) * NY].astype(BF16)
+        packs.append(send(A_PACK + k, psend.at[k], precv.at[r], 0, SPAN - r))
+    hear(0, 2)
+    tell(1, (1, 0), (-1, 0))
+    hear(2, 2)
+    tell(3, (0, 8), (0, -8))
+    precv[SPAN] = pacc[:, SPAN * NY : (SPAN + 1) * NY].astype(BF16)
 
     rowm, colm = iota((24, 96), 0), iota((24, 96), 1)
     low_x, high_x = hats(colm & 15)
     order = rowm >> 3
     weight_x = jnp.where(order == 0, low_x * low_x, jnp.where(order == 1, low_x * high_x, high_x * high_x))
     weight_x = jnp.where((rowm & 7) == (colm >> 4), weight_x, 0.0)
+    weights_x = jnp.concatenate(halves(weight_x), axis=0)
 
     def moments(z, _):
         total = [[None] * 6 for _ in range(3)]
@@ -228,7 +270,11 @@
                     term = product * weight
                     total[m][k] = term if i == 0 else total[m][k] + term
         for m in range(3):
-            rows = jnp.dot(weight_x, jnp.concatenate(total[m], axis=0), precision=EXACT, preferred_element_type=F32)
+            parts = [
+                jnp.dot(weights_x, part, preferred_element_type=F32)
+                for part in halves(jnp.concatenate(total[m], axis=0))
+            ]
+            rows = (parts[1][:24] + parts[0][24:]) + parts[0][:24]
             xrow[pl.ds(pl.multiple_of((z * 3 + m) * 24, 24), 24), :] = rows
         return 0
 
@@ -245,7 +291,7 @@
             jnp.where(starts, low_y * low_y, 0.0) + jnp.where(closes, high_y * high_y, 0.0),
         ),
     ) * (1.0 / VOL)
-    yrow = jnp.dot(xrow[...], weight_y, precision=EXACT, preferred_element_type=F32)
+    yrow = near_exact(xrow[...], weight_y)
     on = [block == z for z in range(EZ + 1)]
     for m in range(3):
         for dy in range(3):
@@ -266,17 +312,6 @@
         send(A_STENCIL + 1, ss, sy, 0, 1),
         send(A_STENCIL + 2, ss.at[1:3], sxy, 1, 1),
     ]
-
-    for z in range(EZ):
-        def fill_place(b, _):
-            row = b * NY + iota((NY, NY), 0)
-            high = portion[2][z : z + 1]
-            place = jnp.where(row == target0[z : z + 1], 1.0 - high, 0.0)
-            place = place + jnp.where(row == target1[z : z + 1], high, 0.0)
-            qmat[pl.ds(pl.multiple_of(b * NY, NY), NY), z * NY : (z + 1) * NY] = place.astype(BF16)
-            return 0
-
-        lax.fori_loop(0, ROUTES, fill_place, 0)
 
     column = inner - 4
     own = (column >= 0) & (column < EYD) & (block <= EZ)
@@ -404,6 +439,8 @@
         product = jnp.sum(powers[k // 2] * powers[(k + 1) // 2], axis=0, keepdims=True)
         tile = jnp.where(sub == k, product, tile)
     gs[...] = tile
+    hear(1, 2)
+    hear(3, 2)
 
     def to_x(k, _):
         copy(gs, gr.at[k - 1], gssem.at[k - 1], grsem.at[k - 1], k, 0)
@@ -416,8 +453,10 @@
         ).wait()
         return total + gr[k - 1]
 
-    lax.fori_loop(1, nx, to_x, 0)
-    tile = lax.fori_loop(1, nx, from_x, tile)
+    for k in sorted(range(1, nx), key=lambda k: (-min(k, nx - k), k)):
+        to_x(k, 0)
+    for k in range(1, nx):
+        tile = from_x(k, tile)
     hs[...] = tile
 
     def to_y(k, _):
@@ -431,8 +470,10 @@
         ).wait()
         return total + hr[k - 1]
 
-    lax.fori_loop(1, ny, to_y, 0)
-    tile = lax.fori_loop(1, ny, from_y, tile)
+    for k in sorted(range(1, ny), key=lambda k: (-min(k, ny - k), k)):
+        to_y(k, 0)
+    for k in range(1, ny):
+        tile = from_y(k, tile)
     total = jnp.broadcast_to(jnp.sum(tile, axis=1, keepdims=True), (8, NY))
     moment = [total[k : k + 1] for k in range(6)]
 
@@ -467,16 +508,23 @@
 
 def body(nx, ny, reference_image, deformed_image, route, within, xshift, fractions):
     vmem = pl.BlockSpec(memory_space=pltpu.VMEM)
-    smem = pl.BlockSpec(memory_space=pltpu.SMEM)
     half = (NZ, EDGE, NY)
     tile = (8, NY)
     inc, mis = pl.pallas_call(
         lambda *refs: kernel(nx, ny, *refs),
         name="correlate",
         out_shape=(jax.ShapeDtypeStruct(tile, F32), jax.ShapeDtypeStruct(half, F32)),
-        in_specs=[smem] * 4 + [vmem] * 2,
+        in_specs=[pl.BlockSpec(memory_space=pltpu.HBM)] * 6,
         out_specs=(vmem, vmem),
         scratch_shapes=[
+            pltpu.SMEM((1, 1, NEL), jnp.int32),
+            pltpu.SMEM((1, 1, NEL), jnp.int32),
+            pltpu.SMEM((1, 1, NEL), jnp.int32),
+            pltpu.SMEM((1, 3, 1, NEL), jnp.int32),
+            pltpu.VMEM(half, BF16),
+            pltpu.VMEM(half, BF16),
+            pltpu.SemaphoreType.DMA((6,)),
+            pltpu.SemaphoreType.REGULAR((4,)),
             pltpu.VMEM((2,) + half, BF16),
             pltpu.VMEM(tile, jnp.int32),
             pltpu.VMEM((4,) + tile, jnp.int32),
@@ -514,9 +562,9 @@
             pltpu.SemaphoreType.DMA((ny - 1,)),
         ],
         compiler_params=pltpu.CompilerParams(
-            collective_id=0, has_side_effects=True, vmem_limit_bytes=48 << 20
+            collective_id=0, has_side_effects=True, vmem_limit_bytes=63 << 20
         ),
-    )(route, within, xshift, fractions, reference_image, deformed_image)
+    )(route.reshape(1, 1, NEL), within, xshift, fractions.transpose(0, 3, 1, 2), reference_image, deformed_image)
     grid = inc[:3].reshape(3, 8, 16)
     return grid[:, : EZ + 1, None, 4 : 4 + EYD], mis
 

time: 61.7 us -> 60.5 us (0.981)
  local copies, waits for them, and re-layouts: 4.88 us -> 3.31 us
    unnamed x15 -> x3, local copies, waits for them, and re-layouts: 4.72 us -> 2.48 us
    slice x1, local copies, waits for them, and re-layouts: 0.01 us -> 0.68 us  [body(): grid = inc[:3].reshape(3, 8, 16)]
where the time goes in v2:
time: 60.5 us; the launch traced here: 60.4 us
  Pallas kernels  56.4 us (93%)
  local copies, waits for them, and re-layouts  3.31 us (5%)
  between operations  0.64 us (1%)
    pallas_call x1, Pallas kernels, body(): pl.pallas_call(lambda *refs: kernel(nx, ny, *refs), name='correlate', out...  56.4 us
    unnamed x3, local copies, waits for them, and re-layouts  2.48 us

profile of v2, /device:TPU:1, one launch (start us, length us, event | category | flops | bytes accessed | tf_op | source)
XLA Modules:
  0.0 60.4 jit_solution(5717395869402907739)
XLA Ops:
  0.6 56.4 %correlate.1 = (f32[8,128]{1,0:T(8,128)}, f32[64,16,128]{2,1,0:T(8,128)}) custom-call(s32[1,1,32]{2,1,0:T(1,128)} %bitcast.7, s32[1,1,32]{2,1,0:T(1,128)} %refs_1_.1, s32[1,1,32]{2,1,0:T(1,128)} %refs_2_.1, s32[1,3,1,32]{3,2,1,0:T(1,128)} %bitcast.6, bf16[64,16,128]{2,1,0:T(8,128)(2,1)} %refs_4_.1, bf16[64,16,128]{2,1,0:T(8,128)(2,1)} %refs_5_.1), custom_call_target="tpu_custom_call" | custom-call | tf_op jit(solution)/shard_map/correlate/pallas_call | solution.py:513
  57.0 0.7 %slice.6 = f32[3,128]{1,0:T(4,128)S(1)} slice(f32[8,128]{1,0:T(8,128)} %get-tuple-element.4), slice={[0:3], [0:128]} | slice | bytes 3072 | tf_op jit(solution)/shard_map/slice | solution.py:568
  57.7 0.1 reshape.11
  57.8 0.1 slice.8
  57.9 0.6 %copy.9 = f32[3,5,1,8]{3,2,1,0:T(1,128)} copy(f32[3,5,1,8]{3,0,1,2:T(4,128)S(1)} %bitcast.5) | data formatting | bytes 960
  58.5 1.9 %copy.14 = f32[64,16,128]{2,1,0:T(8,128)} copy(f32[64,16,128]{2,1,0:T(8,128)} %get-tuple-element.11) | data formatting | bytes 1048576
  (1 shorter events, 0.0 us)

commit v3 on v2

--- a/solution.py
+++ b/solution.py
@@ -21,20 +21,18 @@
 BF16 = jnp.bfloat16
 EXACT = lax.Precision.HIGHEST
 
-N_TABLE, N_BLOCK, N_FACE_X, N_FACE_Y, N_PACK, N_STENCIL, N_RHS, N_VEC = 4, 2, 2, 2, 4, 3, 11, 8
+N_TABLE, N_BLOCK, N_FACE_X, N_FACE_Y, N_PACK, N_EDGE = 4, 2, 2, 2, 4, 2
 A_TABLE = 0
 A_BLOCK = A_TABLE + N_TABLE
 A_FACE_X = A_BLOCK + N_BLOCK
 A_FACE_Y = A_FACE_X + N_FACE_X
 A_PACK = A_FACE_Y + N_FACE_Y
-A_STENCIL = A_PACK + N_PACK
-A_RHS = A_STENCIL + N_STENCIL
-A_VEC = A_RHS + N_RHS
-A_END = A_VEC + 2 * N_VEC
+A_EDGE = A_PACK + N_PACK
+A_END = A_EDGE + N_EDGE
 
 OTHER_ROUTES = (1, 3, 0, 4)
-RHS_OFFSETS = [(dp, dq) for dp in (-1, 0, 1, 2) for dq in (-1, 0, 1) if (dp, dq) != (0, 0)]
-VEC_OFFSETS = [(dp, dq) for dp in (-1, 0, 1) for dq in (-1, 0, 1) if (dp, dq) != (0, 0)]
+STEPS = ((0, 0), (0, 1), (1, -1), (1, 0), (1, 1))
+HALF = len(STEPS)
 PAIRS = ((0, 0), (1, 1), (2, 2), (0, 1), (0, 2), (1, 2))
 
 
@@ -71,8 +69,8 @@
 def kernel(
     nx, ny, route_hbm, within_hbm, xshift_hbm, fractions_hbm, ref_hbm, dfm_hbm, inc, mis,
     route, within, xshift, fractions, ref, dfm, lsem, gossip,
-    xb, tsend, trecv, fxs, fxr, fys, fyr, pmat, pacc, psend, precv, qmat, grad, refp, xrow, ss, sx, sy, sxy,
-    kk, rrow, rs, rr, vs, vr, gs, gr, hs, hr, ssem, rsem, gssem, grsem, hssem, hrsem,
+    xb, tsend, trecv, fxs, fxr, fys, fyr, pmat, pacc, psend, precv, qmat, grad, refp, xrow, es, er, sg,
+    kd, k1, rrow, rr, vv, hs, hr, ssem, rsem, gssem, grsem, rssem, rrsem, hssem, hrsem,
 ):
     p, q = lax.axis_index("gx"), lax.axis_index("gy")
 
@@ -172,7 +170,10 @@
     target0 = first + inner
     target1 = first + jnp.minimum(inner + 1, EDGE - 1)
 
-    for c in faces_x + faces_y:
+    for c in faces_x:
+        c.wait_recv()
+    tell(0, (1, 0), (-1, 0))
+    for c in faces_y:
         c.wait_recv()
     refp[1 : NZ + 1, 7, :] = fxr[0].astype(F32) * flag(p > 0)
     refp[1 : NZ + 1, 24, :] = fxr[1].astype(F32) * flag(p < nx - 1)
@@ -197,7 +198,6 @@
         return 0
 
     lax.fori_loop(0, NZ // 4, slope, 0)
-    tell(0, (1, 0), (-1, 0))
 
     for z in range(EZ):
         def fill_place(b, _):
@@ -212,7 +212,7 @@
 
     for c in tables:
         c.wait_recv()
-    tell(2, (0, 4), (0, -4))
+    tell(3, (0, 4), (0, -4))
     asked = []
     for r in range(ROUTES):
         if r == SPAN:
@@ -235,6 +235,8 @@
         )
 
     width = EZ * NY
+    hear(0, 2)
+    tell(1, (1, 0), (-1, 0))
     loads[5].wait()
     pacc[...] = jnp.dot(brick_rows(dfm), pmat[width : 2 * width, :], preferred_element_type=F32)
     blocks[1].wait_recv()
@@ -245,11 +247,12 @@
     for k, r in enumerate(OTHER_ROUTES):
         psend[k] = pacc[:, r * NY : (r + 1) * NY].astype(BF16)
         packs.append(send(A_PACK + k, psend.at[k], precv.at[r], 0, SPAN - r))
-    hear(0, 2)
-    tell(1, (1, 0), (-1, 0))
-    hear(2, 2)
-    tell(3, (0, 8), (0, -8))
     precv[SPAN] = pacc[:, SPAN * NY : (SPAN + 1) * NY].astype(BF16)
+
+    hear(1, 2)
+    tell(2, (1, 0), (-1, 0))
+    hear(3, 2)
+    tell(4, (0, 8), (0, -8))
 
     rowm, colm = iota((24, 96), 0), iota((24, 96), 1)
     low_x, high_x = hats(colm & 15)
@@ -293,47 +296,49 @@
     ) * (1.0 / VOL)
     yrow = near_exact(xrow[...], weight_y)
     on = [block == z for z in range(EZ + 1)]
+    mine = [[None] * HALF for _ in range(3)]
     for m in range(3):
-        for dy in range(3):
+        for k, (dz, dy) in enumerate(STEPS):
             def term(z, depth):
                 start = (z * 3 + depth) * 24 + m * 8
-                return yrow[start : start + 8, dy * NY : (dy + 1) * NY]
-
-            zero = jnp.zeros((8, NY), F32)
-            down, same, up = zero, zero, zero
+                return yrow[start : start + 8, (dy + 1) * NY : (dy + 2) * NY]
+
+            total = jnp.zeros((8, NY), F32)
             for z in range(EZ):
-                cross = term(z, 1)
-                up = jnp.where(on[z], cross, up)
-                down = jnp.where(on[z + 1], cross, down)
-                same = same + jnp.where(on[z], term(z, 0), 0.0) + jnp.where(on[z + 1], term(z, 2), 0.0)
-            ss[m, dy], ss[m, 3 + dy], ss[m, 6 + dy] = down, same, up
-    stencils = [
-        send(A_STENCIL, ss.at[1:3], sx, 1, 0),
-        send(A_STENCIL + 1, ss, sy, 0, 1),
-        send(A_STENCIL + 2, ss.at[1:3], sxy, 1, 1),
-    ]
-
+                if dz == 1:
+                    total = jnp.where(on[z], term(z, 1), total)
+                else:
+                    total = total + jnp.where(on[z], term(z, 0), 0.0) + jnp.where(on[z + 1], term(z, 2), 0.0)
+            mine[m][k] = total
+    for m in range(3):
+        for part, ks in enumerate(((0, 1, 2), (3, 4))):
+            upper, lower = jnp.zeros((8, NY), F32), jnp.zeros((8, NY), F32)
+            for k in ks:
+                offset = 5 * (k % 3)
+                spot = (inner >= offset) & (inner < offset + 5)
+                upper = jnp.where(spot, rolled(mine[m][k], offset - 8, 1), upper)
+                lower = jnp.where(spot, rolled(mine[m][k], offset - 4, 1), lower)
+            es[0, m * 2 + part], es[1, m * 2 + part] = upper, lower
+    edges = [send(A_EDGE, es.at[0], er.at[0], 0, 1), send(A_EDGE + 1, es.at[1], er.at[1], 0, -1)]
+    for c in edges:
+        c.wait_recv()
+    for m in range(3):
+        for k in range(HALF):
+            offset, part = 5 * (k % 3), k // 3
+            below = jnp.where(inner < 5, rolled(er[0, m * 2 + part], -offset, 1), 0.0) * flag(q > 0)
+            above = jnp.where(inner >= 12, rolled(er[1, m * 2 + part], 12 - offset, 1), 0.0) * flag(q < ny - 1)
+            sg[p, m * HALF + k] = mine[m][k] + below + above
+    spread = []
+    for k in sorted(range(1, nx), key=lambda k: (-min(k, nx - k), k)):
+        spread.append(copy(sg.at[p], sg.at[p], gssem.at[k - 1], grsem.at[k - 1], k, 0))
+    started.extend(spread)
+
+    for c in packs:
+        c.wait_recv()
+    taken = jnp.concatenate([precv[r] for r in range(ROUTES)], axis=1)
     column = inner - 4
-    own = (column >= 0) & (column < EYD) & (block <= EZ)
-    has_x, has_y = flag(p > 0), flag(q > 0)
-    for c in stencils:
-        c.wait_recv()
-
-    def fold(from_y):
-        return jnp.where(inner < 8, rolled(from_y, -8, 1), 0.0) * has_y
-
-    for t in range(9):
-        here0 = ss[0, t] + fold(sy[0, t])
-        here1 = ss[1, t] + fold(sy[1, t])
-        back1 = (sx[0, t] + fold(sxy[0, t])) * has_x
-        back2 = (sx[1, t] + fold(sxy[1, t])) * has_x
-        kk[0, t] = jnp.where(own, back1, 0.0)
-        kk[1, t] = jnp.where(own, here0 + back2, 0.0)
-        kk[2, t] = jnp.where(own, here1, 0.0)
-
-    for c in packs:
-        c.wait_recv()
-    taken = jnp.concatenate([precv[r] for r in range(ROUTES)], axis=1)
+    own = (column >= 0) & (column < EYD) & (block <= EZ) & (sub < 3)
+    inside = (q * EYD + column < ny * EYD) & (sub < 3)
     fetched = jnp.dot(taken, qmat[...], preferred_element_type=F32)
     row8, col16 = iota((8, EDGE), 0), iota((8, EDGE), 1)
     low_j, high_j = hats(iota((EDGE, 1), 0))
@@ -371,92 +376,79 @@
         for m in range(2):
             start = (z * 2 + m) * 8
             tile = tile + jnp.where(on[z + m], nodes[start : start + 8], 0.0)
-    rs[...] = tile
-
-    def gathered(mine, arrived, dp):
-        total = mine
-        for dq, shift, keep in ((1, 8, inner >= 8), (-1, -8, inner < 8)):
-            inside = flag((q + dq >= 0) & (q + dq < ny))
-            total = total + jnp.where(keep, rolled(arrived(dp, dq), shift, 1), 0.0) * inside
-        return total * flag((p + dp >= 0) & (p + dp < nx))
-
-    sent = [send(A_RHS + k, rs, rr.at[k], -dp, -dq) for k, (dp, dq) in enumerate(
-        [(-dp, -dq) for dp, dq in RHS_OFFSETS])]
+    rr[1, p] = tile
+    hear(2, 2)
+    sent = []
+    for k in sorted(range(nx), key=lambda k: (-min(k, nx - k), k)):
+        for dq in (1, -1, 0):
+            if k or dq:
+                number = k * 3 + 1 - dq
+                sent.append(copy(rr.at[1, p], rr.at[1 - dq, p], rssem.at[number], rrsem.at[number], k, dq))
+    started.extend(sent)
+
+    for c in spread:
+        c.wait_recv()
+    for x in range(nx):
+        for k, (dz, dy) in enumerate(STEPS):
+            level, cross = sg[x, k], sg[x, HALF + k]
+            if x > 0:
+                level = level + sg[x - 1, 2 * HALF + k]
+            kd[x, 4 + k], k1[x, 4 + k] = level, cross
+            if k:
+                shift = dz * 16 + dy
+                kd[x, 4 - k], k1[x, 4 - k] = rolled(level, shift, 1), rolled(cross, shift, 1)
+
     for c in sent:
         c.wait_recv()
-
-    def rhs_from(dp, dq):
-        return rs[...] if (dp, dq) == (0, 0) else rr[RHS_OFFSETS.index((-dp, -dq))]
-
-    around = {dp: gathered(rhs_from(dp, 0), rhs_from, dp) for dp in (-2, -1, 0, 1)}
-    first3 = sub < 3
-    inside_y = q * EYD + column < ny * EYD
-    vector = []
-    for dp in (-1, 0, 1):
-        whole = around[dp] + rolled(around[dp - 1], 4, 0)
-        vector.append(jnp.where(first3 & inside_y, whole, 0.0) * flag((p + dp >= 0) & (p + dp < nx)))
-
-    def apply(vector):
-        straight, crossed = jnp.zeros((8, NY), F32), jnp.zeros((8, NY), F32)
-        for dx in range(3):
-            u = [vector[dx][c : c + 1] for c in range(3)]
+    below, above = flag(q > 0), flag(q < ny - 1)
+    tiles = []
+    for x in range(nx):
+        from_below = jnp.where(inner < 8, rolled(rr[0, x], -8, 1), 0.0) * below
+        from_above = jnp.where(inner >= 8, rolled(rr[2, x], 8, 1), 0.0) * above
+        tiles.append(rr[1, x] + from_below + from_above)
+    for x in range(nx):
+        whole = tiles[x] + rolled(tiles[x - 1], 4, 0) if x else tiles[x]
+        vv[0, x] = jnp.where(inside, whole, 0.0)
+
+    for step in range(3):
+        straight = [jnp.zeros((8, NY), F32) for _ in range(nx)]
+        crossed = [jnp.zeros((8, NY), F32) for _ in range(nx)]
+        for x in range(nx):
+            u = [vv[step, x, c : c + 1, :] for c in range(3)]
             second = jnp.where(sub == 0, u[0], jnp.where((sub == 1) | (sub == 3), u[1], u[2]))
             third = jnp.where(sub == 5, u[1], u[0])
             for t in range(9):
                 shift = -((t // 3 - 1) * 16 + t % 3 - 1)
-                weight = kk[dx, t]
-                straight = straight + weight * rolled(second, shift, 1)
-                crossed = crossed + weight * rolled(third, shift, 1)
-        s = [straight[k : k + 1] for k in range(6)]
-        out = [
-            s[0] + s[3] + s[4],
-            s[1] + s[5] + crossed[3:4],
-            s[2] + crossed[4:5] + crossed[5:6],
-        ]
-        image = jnp.where(sub == 0, out[0], jnp.where(sub == 1, out[1], out[2]))
-        return jnp.where(own & first3, image + LAMBDA * vector[1], 0.0)
-
-    powers = [jnp.where(own, vector[1], 0.0)]
-    for step in range(3):
-        image = apply(vector)
-        powers.append(image)
-        if step < 2:
-            vs[step] = image
-            sent = [
-                send(A_VEC + step * N_VEC + k, vs.at[step], vr.at[step, k], dp, dq)
-                for k, (dp, dq) in enumerate(VEC_OFFSETS)
+                moved, other = rolled(second, shift, 1), rolled(third, shift, 1)
+                level, cross = kd[x, t], k1[x, t]
+                straight[x] = straight[x] + level * moved
+                crossed[x] = crossed[x] + level * other
+                if x + 1 < nx:
+                    straight[x + 1] = straight[x + 1] + cross * moved
+                    crossed[x + 1] = crossed[x + 1] + cross * other
+                if x > 0:
+                    before = k1[x - 1, t]
+                    straight[x - 1] = straight[x - 1] + before * moved
+                    crossed[x - 1] = crossed[x - 1] + before * other
+        for x in range(nx):
+            a, b = straight[x], crossed[x]
+            out = [
+                a[0:1] + a[3:4] + a[4:5],
+                a[1:2] + a[5:6] + b[3:4],
+                a[2:3] + b[4:5] + b[5:6],
             ]
-            for c in sent:
-                c.wait_recv()
-
-            def arrived(dp, dq):
-                return vr[step, VEC_OFFSETS.index((-dp, -dq))]
-
-            vector = [gathered(image if dp == 0 else arrived(dp, 0), arrived, dp) for dp in (-1, 0, 1)]
+            image = jnp.where(sub == 0, out[0], jnp.where(sub == 1, out[1], out[2]))
+            vv[step + 1, x] = jnp.where(inside, image + LAMBDA * vv[step, x], 0.0)
 
     tile = jnp.zeros((8, NY), F32)
     for k in range(6):
-        product = jnp.sum(powers[k // 2] * powers[(k + 1) // 2], axis=0, keepdims=True)
+        product = jnp.zeros((8, NY), F32)
+        for x in range(nx):
+            product = product + vv[k // 2, x] * vv[(k + 1) // 2, x]
+        product = jnp.sum(jnp.where(own, product, 0.0), axis=0, keepdims=True)
         tile = jnp.where(sub == k, product, tile)
-    gs[...] = tile
-    hear(1, 2)
-    hear(3, 2)
-
-    def to_x(k, _):
-        copy(gs, gr.at[k - 1], gssem.at[k - 1], grsem.at[k - 1], k, 0)
-        return 0
-
-    def from_x(k, total):
-        pltpu.make_async_remote_copy(
-            src_ref=gs, dst_ref=gr.at[k - 1], send_sem=gssem.at[k - 1], recv_sem=grsem.at[k - 1],
-            device_id=at(k, 0), device_id_type=MESH,
-        ).wait()
-        return total + gr[k - 1]
-
-    for k in sorted(range(1, nx), key=lambda k: (-min(k, nx - k), k)):
-        to_x(k, 0)
-    for k in range(1, nx):
-        tile = from_x(k, tile)
+    hear(4, 2)
+
     hs[...] = tile
 
     def to_y(k, _):
@@ -501,7 +493,7 @@
             norm = after
             widened = direction + [blank]
             direction = [residual[i] + beta * widened[i] for i in range(step + 2)]
-    inc[...] = answer[0] * powers[0] + answer[1] * powers[1] + answer[2] * powers[2]
+    inc[...] = answer[0] * vv[0, p] + answer[1] * vv[1, p] + answer[2] * vv[2, p]
     for c in started:
         c.wait_send()
 
@@ -524,7 +516,7 @@
             pltpu.VMEM(half, BF16),
             pltpu.VMEM(half, BF16),
             pltpu.SemaphoreType.DMA((6,)),
-            pltpu.SemaphoreType.REGULAR((4,)),
+            pltpu.SemaphoreType.REGULAR((5,)),
             pltpu.VMEM((2,) + half, BF16),
             pltpu.VMEM(tile, jnp.int32),
             pltpu.VMEM((4,) + tile, jnp.int32),
@@ -540,24 +532,22 @@
             pltpu.VMEM((3,) + half, BF16),
             pltpu.VMEM((NZ + 2, 32, NY), F32),
             pltpu.VMEM((12 * 24, NY), F32),
-            pltpu.VMEM((3, 9) + tile, F32),
-            pltpu.VMEM((2, 9) + tile, F32),
-            pltpu.VMEM((3, 9) + tile, F32),
-            pltpu.VMEM((2, 9) + tile, F32),
-            pltpu.VMEM((3, 9) + tile, F32),
+            pltpu.VMEM((2, 6) + tile, F32),
+            pltpu.VMEM((2, 6) + tile, F32),
+            pltpu.VMEM((nx, 3 * HALF) + tile, F32),
+            pltpu.VMEM((nx, 9) + tile, F32),
+            pltpu.VMEM((nx, 9) + tile, F32),
             pltpu.VMEM((64, NY), F32),
-            pltpu.VMEM(tile, F32),
-            pltpu.VMEM((N_RHS,) + tile, F32),
-            pltpu.VMEM((2,) + tile, F32),
-            pltpu.VMEM((2, N_VEC) + tile, F32),
-            pltpu.VMEM(tile, F32),
-            pltpu.VMEM((nx - 1,) + tile, F32),
+            pltpu.VMEM((3, nx) + tile, F32),
+            pltpu.VMEM((4, nx) + tile, F32),
             pltpu.VMEM(tile, F32),
             pltpu.VMEM((ny - 1,) + tile, F32),
             pltpu.SemaphoreType.DMA((A_END,)),
             pltpu.SemaphoreType.DMA((A_END,)),
             pltpu.SemaphoreType.DMA((nx - 1,)),
             pltpu.SemaphoreType.DMA((nx - 1,)),
+            pltpu.SemaphoreType.DMA((3 * nx,)),
+            pltpu.SemaphoreType.DMA((3 * nx,)),
             pltpu.SemaphoreType.DMA((ny - 1,)),
             pltpu.SemaphoreType.DMA((ny - 1,)),
         ],

time: 60.5 us -> 48.2 us (0.80)
  Pallas kernels: 56.4 us -> 44.1 us
    pallas_call x1, Pallas kernels: 56.4 us -> 44.1 us  [body(): pl.pallas_call(lambda *refs: kernel(nx, ny, *refs), name='correlate', out...]
where the time goes in v3:
time: 48.2 us; the launch traced here: 48.1 us
  Pallas kernels  44.1 us (91%)
  local copies, waits for them, and re-layouts  3.31 us (7%)
  between operations  0.64 us (1%)
    pallas_call x1, Pallas kernels, body(): pl.pallas_call(lambda *refs: kernel(nx, ny, *refs), name='correlate', out...  44.1 us
    unnamed x3, local copies, waits for them, and re-layouts  2.48 us

profile of v3, /device:TPU:1, one launch (start us, length us, event | category | flops | bytes accessed | tf_op | source)
XLA Modules:
  0.0 48.1 jit_solution(17340522848984157077)
XLA Ops:
  0.6 44.1 %correlate.1 = (f32[8,128]{1,0:T(8,128)}, f32[64,16,128]{2,1,0:T(8,128)}) custom-call(s32[1,1,32]{2,1,0:T(1,128)} %bitcast.7, s32[1,1,32]{2,1,0:T(1,128)} %refs_1_.1, s32[1,1,32]{2,1,0:T(1,128)} %refs_2_.1, s32[1,3,1,32]{3,2,1,0:T(1,128)} %bitcast.6, bf16[64,16,128]{2,1,0:T(8,128)(2,1)} %refs_4_.1, bf16[64,16,128]{2,1,0:T(8,128)(2,1)} %refs_5_.1), custom_call_target="tpu_custom_call" | custom-call | tf_op jit(solution)/shard_map/correlate/pallas_call | solution.py:505
  44.7 0.7 %slice.6 = f32[3,128]{1,0:T(4,128)S(1)} slice(f32[8,128]{1,0:T(8,128)} %get-tuple-element.4), slice={[0:3], [0:128]} | slice | bytes 3072 | tf_op jit(solution)/shard_map/slice | solution.py:558
  45.4 0.1 reshape.11
  45.5 0.1 slice.8
  45.6 0.6 %copy.9 = f32[3,5,1,8]{3,2,1,0:T(1,128)} copy(f32[3,5,1,8]{3,0,1,2:T(4,128)S(1)} %bitcast.5) | data formatting | bytes 960
  46.2 1.9 %copy.14 = f32[64,16,128]{2,1,0:T(8,128)} copy(f32[64,16,128]{2,1,0:T(8,128)} %get-tuple-element.11) | data formatting | bytes 1048576
  (1 shorter events, 0.0 us)

commit v4 on v3

--- a/solution.py
+++ b/solution.py
@@ -30,7 +30,7 @@
 A_EDGE = A_PACK + N_PACK
 A_END = A_EDGE + N_EDGE
 
-OTHER_ROUTES = (1, 3, 0, 4)
+OTHER_ROUTES = (0, 4, 1, 3)
 STEPS = ((0, 0), (0, 1), (1, -1), (1, 0), (1, 1))
 HALF = len(STEPS)
 PAIRS = ((0, 0), (1, 1), (2, 2), (0, 1), (0, 2), (1, 2))
@@ -110,9 +110,6 @@
 
     def hear(number, count):
         pl.semaphore_wait(gossip.at[number], count)
-
-    pl.semaphore_wait(barrier, len(near))
-    blocks = [send(A_BLOCK, dfm_hbm, xb.at[1], -1, 0), send(A_BLOCK + 1, dfm_hbm, xb.at[0], 1, 0)]
 
     lane, sub = iota((8, NY), 1), iota((8, NY), 0)
     block, inner = lane >> 4, lane & 15
@@ -129,9 +126,6 @@
         wanted = jnp.where(hit & (count == block), inner + code, wanted)
         count = count + jnp.where(hit, 1, 0)
     tsend[...] = wanted
-    tables = [
-        send(A_TABLE + k, tsend, trecv.at[k], 0, r - SPAN) for k, r in enumerate(OTHER_ROUTES)
-    ]
 
     loads[4].wait()
     refp[0] = jnp.zeros((32, NY), F32)
@@ -139,20 +133,26 @@
     refp[1 : NZ + 1, 8:24, :] = ref[...].astype(F32)
     fxs[0] = refp[1 : NZ + 1, 8, :].astype(BF16)
     fxs[1] = refp[1 : NZ + 1, 23, :].astype(BF16)
-    faces_x = [
-        send(A_FACE_X, fxs.at[0], fxr.at[1], -1, 0),
-        send(A_FACE_X + 1, fxs.at[1], fxr.at[0], 1, 0),
-    ]
     rows16, lanes16 = iota((16, NY), 0), iota((16, NY), 1)
     pick = ((rows16 == 0) & (lanes16 == 0)) | ((rows16 == 1) & (lanes16 == NY - 1))
     fys[...] = lax.dot_general(
         jnp.where(pick, 1.0, 0.0).astype(BF16), ref[...].reshape(NZ * EDGE, NY),
         (((1,), (1,)), ((), ())), preferred_element_type=F32,
     ).astype(BF16)
+
+    pl.semaphore_wait(barrier, len(near))
     faces_y = [
         send(A_FACE_Y, fys, fyr.at[1], 0, -1),
         send(A_FACE_Y + 1, fys, fyr.at[0], 0, 1),
     ]
+    tables = [
+        send(A_TABLE + k, tsend, trecv.at[k], 0, r - SPAN) for k, r in enumerate(OTHER_ROUTES)
+    ]
+    faces_x = [
+        send(A_FACE_X, fxs.at[0], fxr.at[1], -1, 0),
+        send(A_FACE_X + 1, fxs.at[1], fxr.at[0], 1, 0),
+    ]
+    blocks = [send(A_BLOCK, dfm_hbm, xb.at[1], -1, 0), send(A_BLOCK + 1, dfm_hbm, xb.at[0], 1, 0)]
 
     loads[3].wait()
     element = sub * EYD + block
@@ -170,6 +170,45 @@
     target0 = first + inner
     target1 = first + jnp.minimum(inner + 1, EDGE - 1)
 
+    for z in range(EZ):
+        def fill_place(b, _):
+            row = b * NY + iota((NY, NY), 0)
+            high = portion[2][z : z + 1]
+            place = jnp.where(row == target0[z : z + 1], 1.0 - high, 0.0)
+            place = place + jnp.where(row == target1[z : z + 1], high, 0.0)
+            qmat[pl.ds(pl.multiple_of(b * NY, NY), NY), z * NY : (z + 1) * NY] = place.astype(BF16)
+            return 0
+
+        lax.fori_loop(0, ROUTES, fill_place, 0)
+
+    for c in tables:
+        c.wait_recv()
+    tell(3, (0, 4), (0, -4))
+    asked = []
+    for r in range(ROUTES):
+        if r == SPAN:
+            asked.append(wanted[r : r + 1])
+        else:
+            k = OTHER_ROUTES.index(r)
+            asked.append(trecv[k, r : r + 1, :])
+    asked = jnp.concatenate(asked, axis=1)
+
+    def fill_pack(b, _):
+        row = b * NY + iota((NY, ROUTES * NY), 0)
+        pmat[pl.ds(pl.multiple_of(b * NY, NY), NY), :] = jnp.where(row == asked, 1.0, 0.0).astype(BF16)
+        return 0
+
+    lax.fori_loop(0, 3 * EZ, fill_pack, 0)
+
+    def brick_rows(source):
+        return jnp.concatenate(
+            [source[z * EDGE : (z + 1) * EDGE].reshape(EDGE * EDGE, NY) for z in range(EZ)], axis=1
+        )
+
+    width = EZ * NY
+    loads[5].wait()
+    pacc[...] = jnp.dot(brick_rows(dfm), pmat[width : 2 * width, :], preferred_element_type=F32)
+
     for c in faces_x:
         c.wait_recv()
     tell(0, (1, 0), (-1, 0))
@@ -198,61 +237,6 @@
         return 0
 
     lax.fori_loop(0, NZ // 4, slope, 0)
-
-    for z in range(EZ):
-        def fill_place(b, _):
-            row = b * NY + iota((NY, NY), 0)
-            high = portion[2][z : z + 1]
-            place = jnp.where(row == target0[z : z + 1], 1.0 - high, 0.0)
-            place = place + jnp.where(row == target1[z : z + 1], high, 0.0)
-            qmat[pl.ds(pl.multiple_of(b * NY, NY), NY), z * NY : (z + 1) * NY] = place.astype(BF16)
-            return 0
-
-        lax.fori_loop(0, ROUTES, fill_place, 0)
-
-    for c in tables:
-        c.wait_recv()
-    tell(3, (0, 4), (0, -4))
-    asked = []
-    for r in range(ROUTES):
-        if r == SPAN:
-            asked.append(wanted[r : r + 1])
-        else:
-            k = OTHER_ROUTES.index(r)
-            asked.append(trecv[k, r : r + 1, :])
-    asked = jnp.concatenate(asked, axis=1)
-
-    def fill_pack(b, _):
-        row = b * NY + iota((NY, ROUTES * NY), 0)
-        pmat[pl.ds(pl.multiple_of(b * NY, NY), NY), :] = jnp.where(row == asked, 1.0, 0.0).astype(BF16)
-        return 0
-
-    lax.fori_loop(0, 3 * EZ, fill_pack, 0)
-
-    def brick_rows(source):
-        return jnp.concatenate(
-            [source[z * EDGE : (z + 1) * EDGE].reshape(EDGE * EDGE, NY) for z in range(EZ)], axis=1
-        )
-
-    width = EZ * NY
-    hear(0, 2)
-    tell(1, (1, 0), (-1, 0))
-    loads[5].wait()
-    pacc[...] = jnp.dot(brick_rows(dfm), pmat[width : 2 * width, :], preferred_element_type=F32)
-    blocks[1].wait_recv()
-    pacc[...] += jnp.dot(brick_rows(xb[0]), pmat[0:width, :], preferred_element_type=F32)
-    blocks[0].wait_recv()
-    pacc[...] += jnp.dot(brick_rows(xb[1]), pmat[2 * width : 3 * width, :], preferred_element_type=F32)
-    packs = []
-    for k, r in enumerate(OTHER_ROUTES):
-        psend[k] = pacc[:, r * NY : (r + 1) * NY].astype(BF16)
-        packs.append(send(A_PACK + k, psend.at[k], precv.at[r], 0, SPAN - r))
-    precv[SPAN] = pacc[:, SPAN * NY : (SPAN + 1) * NY].astype(BF16)
-
-    hear(1, 2)
-    tell(2, (1, 0), (-1, 0))
-    hear(3, 2)
-    tell(4, (0, 8), (0, -8))
 
     rowm, colm = iota((24, 96), 0), iota((24, 96), 1)
     low_x, high_x = hats(colm & 15)
@@ -320,6 +304,22 @@
                 lower = jnp.where(spot, rolled(mine[m][k], offset - 4, 1), lower)
             es[0, m * 2 + part], es[1, m * 2 + part] = upper, lower
     edges = [send(A_EDGE, es.at[0], er.at[0], 0, 1), send(A_EDGE + 1, es.at[1], er.at[1], 0, -1)]
+    hear(0, 2)
+    tell(1, (1, 0), (-1, 0))
+    blocks[1].wait_recv()
+    pacc[...] += jnp.dot(brick_rows(xb[0]), pmat[0:width, :], preferred_element_type=F32)
+    blocks[0].wait_recv()
+    pacc[...] += jnp.dot(brick_rows(xb[1]), pmat[2 * width : 3 * width, :], preferred_element_type=F32)
+    packs = []
+    for k, r in enumerate(OTHER_ROUTES):
+        psend[k] = pacc[:, r * NY : (r + 1) * NY].astype(BF16)
+        packs.append(send(A_PACK + k, psend.at[k], precv.at[r], 0, SPAN - r))
+    precv[SPAN] = pacc[:, SPAN * NY : (SPAN + 1) * NY].astype(BF16)
+    hear(1, 2)
+    tell(2, (1, 0), (-1, 0))
+    hear(3, 2)
+    tell(4, (0, 8), (0, -8))
+
     for c in edges:
         c.wait_recv()
     for m in range(3):

time: 48.2 us -> 45.3 us (0.940)
  Pallas kernels: 44.1 us -> 41.2 us
    pallas_call x1, Pallas kernels: 44.1 us -> 41.2 us  [body(): pl.pallas_call(lambda *refs: kernel(nx, ny, *refs), name='correlate', out...]
where the time goes in v4:
time: 45.3 us; the launch traced here: 45.1 us
  Pallas kernels  41.2 us (91%)
  local copies, waits for them, and re-layouts  3.31 us (7%)
  between operations  0.64 us (1%)
    pallas_call x1, Pallas kernels, body(): pl.pallas_call(lambda *refs: kernel(nx, ny, *refs), name='correlate', out...  41.2 us
    unnamed x3, local copies, waits for them, and re-layouts  2.48 us

profile of v4, /device:TPU:1, one launch (start us, length us, event | category | flops | bytes accessed | tf_op | source)
XLA Modules:
  0.0 45.1 jit_solution(9721266118909657894)
XLA Ops:
  0.6 41.2 %correlate.1 = (f32[8,128]{1,0:T(8,128)}, f32[64,16,128]{2,1,0:T(8,128)}) custom-call(s32[1,1,32]{2,1,0:T(1,128)} %bitcast.7, s32[1,1,32]{2,1,0:T(1,128)} %refs_1_.1, s32[1,1,32]{2,1,0:T(1,128)} %refs_2_.1, s32[1,3,1,32]{3,2,1,0:T(1,128)} %bitcast.6, bf16[64,16,128]{2,1,0:T(8,128)(2,1)} %refs_4_.1, bf16[64,16,128]{2,1,0:T(8,128)(2,1)} %refs_5_.1), custom_call_target="tpu_custom_call" | custom-call | tf_op jit(solution)/shard_map/correlate/pallas_call | solution.py:505
  41.8 0.7 %slice.6 = f32[3,128]{1,0:T(4,128)S(1)} slice(f32[8,128]{1,0:T(8,128)} %get-tuple-element.4), slice={[0:3], [0:128]} | slice | bytes 3072 | tf_op jit(solution)/shard_map/slice | solution.py:558
  42.5 0.1 reshape.11
  42.6 0.1 slice.8
  42.7 0.6 %copy.9 = f32[3,5,1,8]{3,2,1,0:T(1,128)} copy(f32[3,5,1,8]{3,0,1,2:T(4,128)S(1)} %bitcast.5) | data formatting | bytes 960
  43.3 1.9 %copy.14 = f32[64,16,128]{2,1,0:T(8,128)} copy(f32[64,16,128]{2,1,0:T(8,128)} %get-tuple-element.11) | data formatting | bytes 1048576
  (1 shorter events, 0.0 us)

commit v5 on v4

--- a/solution.py
+++ b/solution.py
@@ -1,5 +1,6 @@
 import jax
 import jax.numpy as jnp
+import numpy as np
 from jax import lax
 from jax.experimental import pallas as pl
 from jax.experimental.pallas import tpu as pltpu
@@ -16,6 +17,7 @@
 NZ = 64
 NY = 128
 LAMBDA = 0.05
+LAMBDA_PARTS = (float(np.float32(LAMBDA)), 0.0)
 MESH = pl.DeviceIdType.MESH
 F32 = jnp.float32
 BF16 = jnp.bfloat16
@@ -59,6 +61,77 @@
     a, b = halves(left), halves(right)
     total = jnp.dot(a[0], b[1], preferred_element_type=F32) + jnp.dot(a[1], b[0], preferred_element_type=F32)
     return total + jnp.dot(a[0], b[0], preferred_element_type=F32)
+
+
+def two_sum(a, b):
+    total = a + b
+    part = total - a
+    return total, (a - (total - part)) + (b - part)
+
+
+def quick_sum(a, b):
+    total = a + b
+    return total, b - (total - a)
+
+
+def cut_in_two(a):
+    wide = a * 4097.0
+    high = wide - (wide - a)
+    return high, a - high
+
+
+def two_product(a, b):
+    value = a * b
+    (ah, al), (bh, bl) = cut_in_two(a), cut_in_two(b)
+    return value, ((ah * bh - value) + ah * bl + al * bh) + al * bl
+
+
+def plus(a, b):
+    high, low = two_sum(a[0], b[0])
+    return quick_sum(high, low + a[1] + b[1])
+
+
+def minus(a, b):
+    return plus(a, (-b[0], -b[1]))
+
+
+def times(a, b):
+    high, low = two_product(a[0], b[0])
+    return quick_sum(high, low + (a[0] * b[1] + a[1] * b[0]))
+
+
+def inverse(pivot, scale):
+    sound = pivot[0] > scale[0] * 1e-12
+    safe = (jnp.where(sound, pivot[0], 1.0), jnp.where(sound, pivot[1], 0.0))
+    guess = 1.0 / safe[0]
+    zero = jnp.zeros_like(guess)
+    left = minus((zero + 1.0, zero), times(safe, (guess, zero)))
+    result = quick_sum(guess, guess * left[0])
+    return jnp.where(sound, result[0], 0.0), jnp.where(sound, result[1], 0.0)
+
+
+def best_coefficients(moment, weight):
+    count = 3
+    level = (jnp.full_like(moment[0][0], weight[0]), jnp.full_like(moment[0][0], weight[1]))
+    shifted = [plus(moment[k + 1], times(level, moment[k])) for k in range(2 * count - 1)]
+    matrix = [[shifted[i + j] for j in range(count)] for i in range(count)]
+    right = moment[:count]
+    scale = [matrix[i][i] for i in range(count)]
+    pivots = []
+    for i in range(count):
+        pivots.append(inverse(matrix[i][i], scale[i]))
+        for j in range(i + 1, count):
+            ratio = times(matrix[i][j], pivots[i])
+            for k in range(j, count):
+                matrix[j][k] = minus(matrix[j][k], times(ratio, matrix[i][k]))
+            right[j] = minus(right[j], times(ratio, right[i]))
+    answer = [None] * count
+    for i in reversed(range(count)):
+        value = right[i]
+        for j in range(i + 1, count):
+            value = minus(value, times(matrix[i][j], answer[j]))
+        answer[i] = times(value, pivots[i])
+    return answer
 
 
 def hats(position):
@@ -309,12 +382,17 @@
     blocks[1].wait_recv()
     pacc[...] += jnp.dot(brick_rows(xb[0]), pmat[0:width, :], preferred_element_type=F32)
     blocks[0].wait_recv()
-    pacc[...] += jnp.dot(brick_rows(xb[1]), pmat[2 * width : 3 * width, :], preferred_element_type=F32)
+    last = brick_rows(xb[1])
+
+    def packed(r):
+        part = jnp.dot(last, pmat[2 * width : 3 * width, r * NY : (r + 1) * NY], preferred_element_type=F32)
+        return (pacc[:, r * NY : (r + 1) * NY] + part).astype(BF16)
+
     packs = []
     for k, r in enumerate(OTHER_ROUTES):
-        psend[k] = pacc[:, r * NY : (r + 1) * NY].astype(BF16)
+        psend[k] = packed(r)
         packs.append(send(A_PACK + k, psend.at[k], precv.at[r], 0, SPAN - r))
-    precv[SPAN] = pacc[:, SPAN * NY : (SPAN + 1) * NY].astype(BF16)
+    precv[SPAN] = packed(SPAN)
     hear(1, 2)
     tell(2, (1, 0), (-1, 0))
     hear(3, 2)
@@ -438,64 +516,48 @@
                 a[2:3] + b[4:5] + b[5:6],
             ]
             image = jnp.where(sub == 0, out[0], jnp.where(sub == 1, out[1], out[2]))
-            vv[step + 1, x] = jnp.where(inside, image + LAMBDA * vv[step, x], 0.0)
-
-    tile = jnp.zeros((8, NY), F32)
+            vv[step + 1, x] = jnp.where(inside, image, 0.0)
+
+    zero = jnp.zeros((8, NY), F32)
+    tile = zero
     for k in range(6):
-        product = jnp.zeros((8, NY), F32)
+        high, low = zero, zero
         for x in range(nx):
-            product = product + vv[k // 2, x] * vv[(k + 1) // 2, x]
-        product = jnp.sum(jnp.where(own, product, 0.0), axis=0, keepdims=True)
-        tile = jnp.where(sub == k, product, tile)
+            value, rest = two_product(vv[k // 2, x], vv[(k + 1) // 2, x])
+            high, lost = two_sum(high, value)
+            low = low + (lost + rest)
+        value, lost = two_sum(high[0:1], high[1:2])
+        value, more = two_sum(value, high[2:3])
+        rest = (low[0:1] + low[1:2]) + (low[2:3] + (lost + more))
+        owned = own[0:1]
+        both = jnp.where(owned, value, 0.0) + rolled(jnp.where(owned, rest, 0.0), 8, 1)
+        tile = jnp.where(sub == k, both, tile)
     hear(4, 2)
-
     hs[...] = tile
 
-    def to_y(k, _):
-        copy(hs, hr.at[k - 1], hssem.at[k - 1], hrsem.at[k - 1], 0, k)
-        return 0
-
-    def from_y(k, total):
-        pltpu.make_async_remote_copy(
-            src_ref=hs, dst_ref=hr.at[k - 1], send_sem=hssem.at[k - 1], recv_sem=hrsem.at[k - 1],
-            device_id=at(0, k), device_id_type=MESH,
-        ).wait()
-        return total + hr[k - 1]
-
+    sums = {}
     for k in sorted(range(1, ny), key=lambda k: (-min(k, ny - k), k)):
-        to_y(k, 0)
-    for k in range(1, ny):
-        tile = from_y(k, tile)
-    total = jnp.broadcast_to(jnp.sum(tile, axis=1, keepdims=True), (8, NY))
-    moment = [total[k : k + 1] for k in range(6)]
-
-    def product(a, b, more):
-        value = 0.0
-        for i, left in enumerate(a):
-            for j, right in enumerate(b):
-                value = value + left * right * moment[i + j + more]
-        return value
-
-    blank, unit = jnp.zeros((1, NY), F32), jnp.ones((1, NY), F32)
-    answer, residual, direction = [blank] * 3, [unit], [unit]
-    norm = moment[0]
-    for step in range(3):
-        bend = product(direction, direction, 1)
-        alpha = norm / bend
-        answer = [answer[i] + alpha * direction[i] if i < len(direction) else answer[i] for i in range(3)]
-        if step < 2:
-            grown = residual + [blank]
-            residual = [
-                grown[i] - alpha * direction[i - 1] if i > 0 else grown[i] for i in range(step + 2)
-            ]
-            after = product(residual, residual, 0)
-            beta = after / norm
-            norm = after
-            widened = direction + [blank]
-            direction = [residual[i] + beta * widened[i] for i in range(step + 2)]
-    inc[...] = answer[0] * vv[0, p] + answer[1] * vv[1, p] + answer[2] * vv[2, p]
+        sums[k] = copy(hs, hr.at[k - 1], hssem.at[k - 1], hrsem.at[k - 1], 0, k)
     for c in started:
         c.wait_send()
+    rest = zero
+    for k in sorted(range(1, ny), key=lambda k: (min(k, ny - k), k)):
+        sums[k].wait_recv()
+        tile, lost = two_sum(tile, hr[k - 1])
+        rest = rest + lost
+    for shift in (64, 32, 16, 8, 4, 2, 1):
+        tile, lost = two_sum(tile, rolled(tile, shift, 1))
+        rest = (rest + rolled(rest, shift, 1)) + lost
+    tile, rest = quick_sum(tile, rest)
+
+    moment = [(tile[k : k + 1], rest[k : k + 1]) for k in range(6)]
+    answer = [high for high, low in best_coefficients(moment, LAMBDA_PARTS)]
+    for k in range(1, ny):
+        sums[k].wait_send()
+    found = answer[0] * vv[0, p] + answer[1] * vv[1, p] + answer[2] * vv[2, p]
+    for c in range(3):
+        for z in range(EZ + 1):
+            inc[c, z, 0:1, :] = found[c : c + 1, z * 16 + 4 : z * 16 + 4 + EYD]
 
 
 def body(nx, ny, reference_image, deformed_image, route, within, xshift, fractions):
@@ -505,7 +567,7 @@
     inc, mis = pl.pallas_call(
         lambda *refs: kernel(nx, ny, *refs),
         name="correlate",
-        out_shape=(jax.ShapeDtypeStruct(tile, F32), jax.ShapeDtypeStruct(half, F32)),
+        out_shape=(jax.ShapeDtypeStruct((3, EZ + 1, 1, EYD), F32), jax.ShapeDtypeStruct(half, F32)),
         in_specs=[pl.BlockSpec(memory_space=pltpu.HBM)] * 6,
         out_specs=(vmem, vmem),
         scratch_shapes=[
@@ -555,8 +617,7 @@
             collective_id=0, has_side_effects=True, vmem_limit_bytes=63 << 20
         ),
     )(route.reshape(1, 1, NEL), within, xshift, fractions.transpose(0, 3, 1, 2), reference_image, deformed_image)
-    grid = inc[:3].reshape(3, 8, 16)
-    return grid[:, : EZ + 1, None, 4 : 4 + EYD], mis
+    return inc, mis
 
 
 def solution(mesh):

time: 45.3 us -> 45.9 us (1.013)
  Pallas kernels: 41.2 us -> 42 us
    pallas_call x1, Pallas kernels: 41.2 us -> 42 us  [body(): pl.pallas_call(lambda *refs: kernel(nx, ny, *refs), name='correlate', out...]
    slice x2 -> x0, local copies, waits for them, and re-layouts: 0.75 us -> none  [the longest x1 0.68 us: body(): grid = inc[:3].reshape(3, 8, 16)]
    unnamed x3 -> x2, local copies, waits for them, and re-layouts: 2.48 us -> 3.16 us
where the time goes in v5:
time: 45.9 us; the launch traced here: 45.8 us
  Pallas kernels  42 us (92%)
  local copies, waits for them, and re-layouts  3.16 us (7%)
  between operations  0.64 us (1%)
    pallas_call x1, Pallas kernels, body(): pl.pallas_call(lambda *refs: kernel(nx, ny, *refs), name='correlate', out...  42 us
    unnamed x2, local copies, waits for them, and re-layouts  3.16 us

profile of v5, /device:TPU:1, one launch (start us, length us, event | category | flops | bytes accessed | tf_op | source)
XLA Modules:
  0.0 45.8 jit_solution(12862423472626405485)
XLA Ops:
  0.6 42.0 %correlate.1 = (f32[3,5,1,8]{3,2,1,0:T(1,128)}, f32[64,16,128]{2,1,0:T(8,128)}) custom-call(s32[1,1,32]{2,1,0:T(1,128)} %bitcast.3, s32[1,1,32]{2,1,0:T(1,128)} %refs_1_.1, s32[1,1,32]{2,1,0:T(1,128)} %refs_2_.1, s32[1,3,1,32]{3,2,1,0:T(1,128)} %bitcast.2, bf16[64,16,128]{2,1,0:T(8,128)(2,1)} %refs_4_.1, bf16[64,16,128]{2,1,0:T(8,128)(2,1)} %refs_5_.1), custom_call_target="tpu_custom_call" | custom-call | tf_op jit(solution)/shard_map/correlate/pallas_call | solution.py:567
  42.6 1.3 %copy.10 = f32[3,5,1,8]{3,2,1,0:T(1,128)} copy(f32[3,5,1,8]{3,2,1,0:T(1,128)} %get-tuple-element.4) | data formatting | bytes 960
  43.9 1.9 %copy.11 = f32[64,16,128]{2,1,0:T(8,128)} copy(f32[64,16,128]{2,1,0:T(8,128)} %get-tuple-element.5) | data formatting | bytes 1048576

commit v6 on v5

--- a/solution.py
+++ b/solution.py
@@ -614,9 +614,15 @@
             pltpu.SemaphoreType.DMA((ny - 1,)),
         ],
         compiler_params=pltpu.CompilerParams(
-            collective_id=0, has_side_effects=True, vmem_limit_bytes=63 << 20
+            collective_id=0, has_side_effects=True, vmem_limit_bytes=48 << 20
         ),
-    )(route.reshape(1, 1, NEL), within, xshift, fractions.transpose(0, 3, 1, 2), reference_image, deformed_image)
+    )(*[
+        pltpu.with_memory_space_constraint(array, pltpu.HBM)
+        for array in (
+            route.reshape(1, 1, NEL), within, xshift, fractions.transpose(0, 3, 1, 2),
+            reference_image, deformed_image,
+        )
+    ])
     return inc, mis
 
 

time: 45.9 us -> 43.4 us (0.946)
  local copies, waits for them, and re-layouts: 3.16 us -> 1.39 us
  Pallas kernels: 42 us -> 41.3 us
    unnamed x2, local copies, waits for them, and re-layouts: 3.16 us -> 1.39 us
    pallas_call x1, Pallas kernels: 42 us -> 41.3 us  [body(): pl.pallas_call(lambda *refs: kernel(nx, ny, *refs), name='correlate', out...]
where the time goes in v6:
time: 43.4 us; the launch traced here: 43.3 us
  Pallas kernels  41.3 us (95%)
  local copies, waits for them, and re-layouts  1.39 us (3%)
  between operations  0.64 us (1%)
    pallas_call x1, Pallas kernels, body(): pl.pallas_call(lambda *refs: kernel(nx, ny, *refs), name='correlate', out...  41.3 us
    unnamed x2, local copies, waits for them, and re-layouts  1.39 us

profile of v6, /device:TPU:1, one launch (start us, length us, event | category | flops | bytes accessed | tf_op | source)
XLA Modules:
  0.0 43.3 jit_solution(17456468686828354760)
XLA Ops:
  0.6 41.3 %correlate.1 = (f32[3,5,1,8]{3,2,1,0:T(1,128)S(1)}, f32[64,16,128]{2,1,0:T(8,128)S(1)}) custom-call(s32[1,1,32]{2,1,0:T(1,128)} %bitcast.3, s32[1,1,32]{2,1,0:T(1,128)} %refs_1_.1, s32[1,1,32]{2,1,0:T(1,128)} %refs_2_.1, s32[1,3,1,32]{3,2,1,0:T(1,128)} %bitcast.2, bf16[64,16,128]{2,1,0:T(8,128)(2,1)} %refs_4_.1, bf16[64,16,128]{2,1,0:T(8,128)(2,1)} %refs_5_.1), custom_call_target="tpu_custom_call" | custom-call | tf_op jit(solution)/shard_map/correlate/pallas_call | solution.py:567
  41.9 0.6 %copy.10 = f32[3,5,1,8]{3,2,1,0:T(1,128)} copy(f32[3,5,1,8]{3,2,1,0:T(1,128)S(1)} %get-tuple-element.4) | data formatting | bytes 960
  42.5 0.8 %copy.11 = f32[64,16,128]{2,1,0:T(8,128)} copy(f32[64,16,128]{2,1,0:T(8,128)S(1)} %get-tuple-element.5) | data formatting | bytes 1048576

commit v7 on v6

--- a/solution.py
+++ b/solution.py
@@ -21,7 +21,6 @@
 MESH = pl.DeviceIdType.MESH
 F32 = jnp.float32
 BF16 = jnp.bfloat16
-EXACT = lax.Precision.HIGHEST
 
 N_TABLE, N_BLOCK, N_FACE_X, N_FACE_Y, N_PACK, N_EDGE = 4, 2, 2, 2, 4, 2
 A_TABLE = 0
@@ -33,6 +32,7 @@
 A_END = A_EDGE + N_EDGE
 
 OTHER_ROUTES = (0, 4, 1, 3)
+ARRIVAL = (2, 1, 3, 0, 4)
 STEPS = ((0, 0), (0, 1), (1, -1), (1, 0), (1, 1))
 HALF = len(STEPS)
 PAIRS = ((0, 0), (1, 1), (2, 2), (0, 1), (0, 2), (1, 2))
@@ -119,18 +119,20 @@
     scale = [matrix[i][i] for i in range(count)]
     pivots = []
     for i in range(count):
-        pivots.append(inverse(matrix[i][i], scale[i]))
+        sound = matrix[i][i][0] > scale[i][0] * 1e-12
+        pivots.append(jnp.where(sound, 1.0 / jnp.where(sound, matrix[i][i][0], 1.0), 0.0))
+        exact = inverse(matrix[i][i], scale[i]) if i + 1 < count else None
         for j in range(i + 1, count):
-            ratio = times(matrix[i][j], pivots[i])
+            ratio = times(matrix[i][j], exact)
             for k in range(j, count):
                 matrix[j][k] = minus(matrix[j][k], times(ratio, matrix[i][k]))
             right[j] = minus(right[j], times(ratio, right[i]))
     answer = [None] * count
     for i in reversed(range(count)):
-        value = right[i]
+        value = right[i][0]
         for j in range(i + 1, count):
-            value = minus(value, times(matrix[i][j], answer[j]))
-        answer[i] = times(value, pivots[i])
+            value = value - matrix[i][j][0] * answer[j]
+        answer[i] = value * pivots[i]
     return answer
 
 
@@ -165,7 +167,7 @@
         started.append(c)
         return c
 
-    near = ((1, 0), (-1, 0), (0, 1), (0, -1), (0, 2), (0, -2))
+    near = ((0, 2), (0, -2), (0, 1), (0, -1), (1, 0), (-1, 0))
     barrier = pltpu.get_barrier_semaphore()
     for dp, dq in near:
         pl.semaphore_signal(barrier, inc=1, device_id=at(dp, dq), device_id_type=MESH)
@@ -238,7 +240,10 @@
     slot = jnp.zeros((8, NY), jnp.int32)
     for e in range(NEL):
         slot = slot + jnp.where((element > e) & (own_route == routes[e]), 1, 0)
-    first = (own_route * CAP + slot) * EDGE
+    turn = jnp.zeros((8, NY), jnp.int32)
+    for k, r in enumerate(ARRIVAL):
+        turn = jnp.where(own_route == r, k, turn)
+    first = (turn * CAP + slot) * EDGE
     portion = [part.astype(F32) / EDGE for part in parts]
     target0 = first + inner
     target1 = first + jnp.minimum(inner + 1, EDGE - 1)
@@ -411,13 +416,19 @@
         spread.append(copy(sg.at[p], sg.at[p], gssem.at[k - 1], grsem.at[k - 1], k, 0))
     started.extend(spread)
 
-    for c in packs:
-        c.wait_recv()
-    taken = jnp.concatenate([precv[r] for r in range(ROUTES)], axis=1)
     column = inner - 4
     own = (column >= 0) & (column < EYD) & (block <= EZ) & (sub < 3)
     inside = (q * EYD + column < ny * EYD) & (sub < 3)
-    fetched = jnp.dot(taken, qmat[...], preferred_element_type=F32)
+    pacc[:, : EZ * NY] = jnp.dot(precv[SPAN], qmat[0:NY, :], preferred_element_type=F32)
+
+    def placed(at, pair):
+        for r in pair:
+            packs[OTHER_ROUTES.index(r)].wait_recv()
+        bricks = jnp.concatenate([precv[r] for r in pair], axis=1)
+        return jnp.dot(bricks, qmat[at * NY : (at + 2) * NY, :], preferred_element_type=F32)
+
+    pacc[:, : EZ * NY] += placed(1, ARRIVAL[1:3])
+    fetched = pacc[:, : EZ * NY] + placed(3, ARRIVAL[3:5])
     row8, col16 = iota((8, EDGE), 0), iota((8, EDGE), 1)
     low_j, high_j = hats(iota((EDGE, 1), 0))
     for z in range(EZ):
@@ -448,7 +459,9 @@
     weight_y = (
         jnp.where(row_y == node_y, low_y, 0.0) + jnp.where(row_y + 1 == node_y, high_y, 0.0)
     ) * (1.0 / VOL)
-    nodes = jnp.dot(rrow[...], weight_y, precision=EXACT, preferred_element_type=F32)
+    weight_y = weight_y.astype(BF16)
+    high, low = halves(rrow[...])
+    nodes = jnp.dot(low, weight_y, preferred_element_type=F32) + jnp.dot(high, weight_y, preferred_element_type=F32)
     tile = jnp.zeros((8, NY), F32)
     for z in range(EZ):
         for m in range(2):
@@ -551,7 +564,7 @@
     tile, rest = quick_sum(tile, rest)
 
     moment = [(tile[k : k + 1], rest[k : k + 1]) for k in range(6)]
-    answer = [high for high, low in best_coefficients(moment, LAMBDA_PARTS)]
+    answer = best_coefficients(moment, LAMBDA_PARTS)
     for k in range(1, ny):
         sums[k].wait_send()
     found = answer[0] * vv[0, p] + answer[1] * vv[1, p] + answer[2] * vv[2, p]

time: 43.4 us -> 42.9 us (0.988)
  Pallas kernels: 41.3 us -> 40.8 us
    pallas_call x1, Pallas kernels: 41.3 us -> 40.8 us  [body(): pl.pallas_call(lambda *refs: kernel(nx, ny, *refs), name='correlate', out...]
where the time goes in v7:
time: 42.9 us; the launch traced here: 42.8 us
  Pallas kernels  40.8 us (95%)
  local copies, waits for them, and re-layouts  1.39 us (3%)
  between operations  0.64 us (1%)
    pallas_call x1, Pallas kernels, body(): pl.pallas_call(lambda *refs: kernel(nx, ny, *refs), name='correlate', out...  40.8 us
    unnamed x2, local copies, waits for them, and re-layouts  1.39 us

profile of v7, /device:TPU:1, one launch (start us, length us, event | category | flops | bytes accessed | tf_op | source)
XLA Modules:
  0.0 42.8 jit_solution(3605726313612491897)
XLA Ops:
  0.6 40.8 %correlate.1 = (f32[3,5,1,8]{3,2,1,0:T(1,128)S(1)}, f32[64,16,128]{2,1,0:T(8,128)S(1)}) custom-call(s32[1,1,32]{2,1,0:T(1,128)} %bitcast.3, s32[1,1,32]{2,1,0:T(1,128)} %refs_1_.1, s32[1,1,32]{2,1,0:T(1,128)} %refs_2_.1, s32[1,3,1,32]{3,2,1,0:T(1,128)} %bitcast.2, bf16[64,16,128]{2,1,0:T(8,128)(2,1)} %refs_4_.1, bf16[64,16,128]{2,1,0:T(8,128)(2,1)} %refs_5_.1), custom_call_target="tpu_custom_call" | custom-call | tf_op jit(solution)/shard_map/correlate/pallas_call | solution.py:580
  41.4 0.6 %copy.10 = f32[3,5,1,8]{3,2,1,0:T(1,128)} copy(f32[3,5,1,8]{3,2,1,0:T(1,128)S(1)} %get-tuple-element.4) | data formatting | bytes 960
  42.0 0.8 %copy.11 = f32[64,16,128]{2,1,0:T(8,128)} copy(f32[64,16,128]{2,1,0:T(8,128)S(1)} %get-tuple-element.5) | data formatting | bytes 1048576

commit v8 on v7

--- a/solution.py
+++ b/solution.py
@@ -259,34 +259,6 @@
 
         lax.fori_loop(0, ROUTES, fill_place, 0)
 
-    for c in tables:
-        c.wait_recv()
-    tell(3, (0, 4), (0, -4))
-    asked = []
-    for r in range(ROUTES):
-        if r == SPAN:
-            asked.append(wanted[r : r + 1])
-        else:
-            k = OTHER_ROUTES.index(r)
-            asked.append(trecv[k, r : r + 1, :])
-    asked = jnp.concatenate(asked, axis=1)
-
-    def fill_pack(b, _):
-        row = b * NY + iota((NY, ROUTES * NY), 0)
-        pmat[pl.ds(pl.multiple_of(b * NY, NY), NY), :] = jnp.where(row == asked, 1.0, 0.0).astype(BF16)
-        return 0
-
-    lax.fori_loop(0, 3 * EZ, fill_pack, 0)
-
-    def brick_rows(source):
-        return jnp.concatenate(
-            [source[z * EDGE : (z + 1) * EDGE].reshape(EDGE * EDGE, NY) for z in range(EZ)], axis=1
-        )
-
-    width = EZ * NY
-    loads[5].wait()
-    pacc[...] = jnp.dot(brick_rows(dfm), pmat[width : 2 * width, :], preferred_element_type=F32)
-
     for c in faces_x:
         c.wait_recv()
     tell(0, (1, 0), (-1, 0))
@@ -382,6 +354,34 @@
                 lower = jnp.where(spot, rolled(mine[m][k], offset - 4, 1), lower)
             es[0, m * 2 + part], es[1, m * 2 + part] = upper, lower
     edges = [send(A_EDGE, es.at[0], er.at[0], 0, 1), send(A_EDGE + 1, es.at[1], er.at[1], 0, -1)]
+    for c in tables:
+        c.wait_recv()
+    tell(3, (0, 4), (0, -4))
+    asked = []
+    for r in range(ROUTES):
+        if r == SPAN:
+            asked.append(wanted[r : r + 1])
+        else:
+            k = OTHER_ROUTES.index(r)
+            asked.append(trecv[k, r : r + 1, :])
+    asked = jnp.concatenate(asked, axis=1)
+
+    def fill_pack(b, _):
+        row = b * NY + iota((NY, ROUTES * NY), 0)
+        pmat[pl.ds(pl.multiple_of(b * NY, NY), NY), :] = jnp.where(row == asked, 1.0, 0.0).astype(BF16)
+        return 0
+
+    lax.fori_loop(0, 3 * EZ, fill_pack, 0)
+
+    def brick_rows(source):
+        return jnp.concatenate(
+            [source[z * EDGE : (z + 1) * EDGE].reshape(EDGE * EDGE, NY) for z in range(EZ)], axis=1
+        )
+
+    width = EZ * NY
+    loads[5].wait()
+    pacc[...] = jnp.dot(brick_rows(dfm), pmat[width : 2 * width, :], preferred_element_type=F32)
+
     hear(0, 2)
     tell(1, (1, 0), (-1, 0))
     blocks[1].wait_recv()

time: 42.9 us -> 42 us (0.979)
  Pallas kernels: 40.8 us -> 39.9 us
    pallas_call x1, Pallas kernels: 40.8 us -> 39.9 us  [body(): pl.pallas_call(lambda *refs: kernel(nx, ny, *refs), name='correlate', out...]
where the time goes in v8:
time: 42 us
  Pallas kernels  39.9 us (95%)
  local copies, waits for them, and re-layouts  1.39 us (3%)
  between operations  0.64 us (2%)
    pallas_call x1, Pallas kernels, body(): pl.pallas_call(lambda *refs: kernel(nx, ny, *refs), name='correlate', out...  39.9 us
    unnamed x2, local copies, waits for them, and re-layouts  1.39 us

profile of v8, /device:TPU:1, one launch (start us, length us, event | category | flops | bytes accessed | tf_op | source)
XLA Modules:
  0.0 42.0 jit_solution(13346351574989847700)
XLA Ops:
  0.6 39.9 %correlate.1 = (f32[3,5,1,8]{3,2,1,0:T(1,128)S(1)}, f32[64,16,128]{2,1,0:T(8,128)S(1)}) custom-call(s32[1,1,32]{2,1,0:T(1,128)} %bitcast.3, s32[1,1,32]{2,1,0:T(1,128)} %refs_1_.1, s32[1,1,32]{2,1,0:T(1,128)} %refs_2_.1, s32[1,3,1,32]{3,2,1,0:T(1,128)} %bitcast.2, bf16[64,16,128]{2,1,0:T(8,128)(2,1)} %refs_4_.1, bf16[64,16,128]{2,1,0:T(8,128)(2,1)} %refs_5_.1), custom_call_target="tpu_custom_call" | custom-call | tf_op jit(solution)/shard_map/correlate/pallas_call | solution.py:580
  40.6 0.6 %copy.10 = f32[3,5,1,8]{3,2,1,0:T(1,128)} copy(f32[3,5,1,8]{3,2,1,0:T(1,128)S(1)} %get-tuple-element.4) | data formatting | bytes 960
  41.2 0.8 %copy.11 = f32[64,16,128]{2,1,0:T(8,128)} copy(f32[64,16,128]{2,1,0:T(8,128)S(1)} %get-tuple-element.5) | data formatting | bytes 1048576

commit v9 on v8

--- a/solution.py
+++ b/solution.py
@@ -400,8 +400,6 @@
     precv[SPAN] = packed(SPAN)
     hear(1, 2)
     tell(2, (1, 0), (-1, 0))
-    hear(3, 2)
-    tell(4, (0, 8), (0, -8))
 
     for c in edges:
         c.wait_recv()
@@ -415,6 +413,9 @@
     for k in sorted(range(1, nx), key=lambda k: (-min(k, nx - k), k)):
         spread.append(copy(sg.at[p], sg.at[p], gssem.at[k - 1], grsem.at[k - 1], k, 0))
     started.extend(spread)
+
+    hear(3, 2)
+    tell(4, (0, 8), (0, -8))
 
     column = inner - 4
     own = (column >= 0) & (column < EYD) & (block <= EZ) & (sub < 3)

time: 42 us -> 42.1 us (level)
  no operation moved by 1% of the time
where the time goes in v9:
time: 42.1 us; the launch traced here: 42 us
  Pallas kernels  39.9 us (95%)
  local copies, waits for them, and re-layouts  1.39 us (3%)
  between operations  0.64 us (2%)
    pallas_call x1, Pallas kernels, body(): pl.pallas_call(lambda *refs: kernel(nx, ny, *refs), name='correlate', out...  39.9 us
    unnamed x2, local copies, waits for them, and re-layouts  1.39 us

profile of v9, /device:TPU:1, one launch (start us, length us, event | category | flops | bytes accessed | tf_op | source)
XLA Modules:
  0.0 42.0 jit_solution(13472832408982092294)
XLA Ops:
  0.6 39.9 %correlate.1 = (f32[3,5,1,8]{3,2,1,0:T(1,128)S(1)}, f32[64,16,128]{2,1,0:T(8,128)S(1)}) custom-call(s32[1,1,32]{2,1,0:T(1,128)} %bitcast.3, s32[1,1,32]{2,1,0:T(1,128)} %refs_1_.1, s32[1,1,32]{2,1,0:T(1,128)} %refs_2_.1, s32[1,3,1,32]{3,2,1,0:T(1,128)} %bitcast.2, bf16[64,16,128]{2,1,0:T(8,128)(2,1)} %refs_4_.1, bf16[64,16,128]{2,1,0:T(8,128)(2,1)} %refs_5_.1), custom_call_target="tpu_custom_call" | custom-call | tf_op jit(solution)/shard_map/correlate/pallas_call | solution.py:581
  40.6 0.6 %copy.10 = f32[3,5,1,8]{3,2,1,0:T(1,128)} copy(f32[3,5,1,8]{3,2,1,0:T(1,128)S(1)} %get-tuple-element.4) | data formatting | bytes 960
  41.2 0.8 %copy.11 = f32[64,16,128]{2,1,0:T(8,128)} copy(f32[64,16,128]{2,1,0:T(8,128)S(1)} %get-tuple-element.5) | data formatting | bytes 1048576
